TPU v7x, 128 devices: a whole 4x4x4 slice. The times are simulated.
128 devices in a mesh: row: 8 (over y, core), col: 16 (over x, z).
Axes of the slice: x: 4, y: 4, z: 4, core: 2. Of those that a mesh axis runs over, the one named last changes fastest.
Arguments:
- marginal: float32 [131072, 128], P(('row', 'col')), may hold values from -6 to 6
- penalty: float32 [128], replicated, may hold values from 0.5 to 8
- ld_diag: float32 [128, 1024, 1024], P(('row', 'col')), may hold values from -0.005 to 1, as said below
- ld_low: float32 [128, 2, 1024, 1024], P(('row', 'col')), may hold values from -0.006 to 0.36
- band: int32 [128], P(('row', 'col')), may hold values from 0 to 2
- genotypes: bfloat16 [5120, 131072], P(None, ('row', 'col')), may hold values from -5 to 5
Outputs:
- effects: float32 [131072, 128], P(('row', 'col'))
- scores: float32 [5120, 128], P(('row', 'col'))
Inputs may be any that keep to these rules, and one draw needn't show every extreme that they name: Each block of ld_diag is symmetric with ones on its diagonal.
All inputs are finite; a program needn't handle non-finite values.
Results may differ from a plain program's by a relative error of at most 0.0023.
The roundings to bfloat16 on the way count: a program that leaves them out, or rounds other values in their place, can miss the bound.
Values sent between devices are 32-bit elements; how exact they have to be, the bound alone decides.
A program may use at most 128 MiB of HBM per device.

v0:
```python
import jax
import jax.numpy as jnp
from jax import lax
from jax.sharding import PartitionSpec as P

ITERS = 3


def from_behind(block, axis, distance):
    devices = range(lax.axis_size(axis))
    route = [(i - distance, i) for i in devices if i - distance in devices]
    return lax.ppermute(block, axis, route)


def body(marginal, penalty, ld_diag, ld_low, band, genotypes):
    highest = lax.Precision.HIGHEST
    position = lax.axis_index(("row", "col"))
    reach = band[0]
    diag_tile = ld_diag[0]
    zeros_block = jnp.zeros(marginal.shape, jnp.float32)

    def squared(vec):
        return lax.psum(jnp.sum(vec * vec, axis=0), ("row", "col"))

    residual = marginal
    effects = jnp.zeros_like(marginal)
    direction = residual
    norm_now = squared(residual)
    for step in range(ITERS):
        apply_vec = direction
        out = (
            jnp.dot(diag_tile, apply_vec, precision=highest, preferred_element_type=jnp.float32)
            + penalty * apply_vec
        )
        for dist in (1, 2):
            tile = ld_low[0, dist - 1]
            active = jnp.logical_and(reach >= dist, position >= dist)
            below = from_behind(apply_vec, ("row", "col"), dist)
            out = out + lax.cond(
                active,
                lambda: jnp.dot(tile, below, precision=highest, preferred_element_type=jnp.float32),
                lambda: zeros_block,
            )
            upper = lax.cond(
                active,
                lambda: lax.dot_general(
                    tile,
                    apply_vec,
                    (((0,), (0,)), ((), ())),
                    precision=highest,
                    preferred_element_type=jnp.float32,
                ),
                lambda: zeros_block,
            )
            out = out + from_behind(upper, ("row", "col"), -dist)
        alpha = norm_now / lax.psum(jnp.sum(direction * out, axis=0), ("row", "col"))
        effects = effects + alpha * direction
        residual = residual - alpha * out
        norm_next = squared(residual)
        direction = residual + norm_next / norm_now * direction
        norm_now = norm_next
    rounded = effects.astype(jnp.bfloat16)
    partial_scores = jnp.dot(genotypes, rounded, preferred_element_type=jnp.float32)
    scores = lax.psum_scatter(partial_scores, ("row", "col"), scatter_dimension=0, tiled=True)
    return (effects, scores)


def solution(mesh):
    placed = (
        P(("row", "col"), None),
        P(),
        P(("row", "col"), None, None),
        P(("row", "col"), None, None, None),
        P(("row", "col")),
        P(None, ("row", "col")),
    )
    return jax.shard_map(
        body,
        mesh=mesh,
        in_specs=placed,
        out_specs=(P(("row", "col"), None), P(("row", "col"), None)),
        check_vma=False,
    )
```

profile of v0, /device:TPU:0, one launch (start us, length us, event | category | flops | bytes accessed | tf_op | source)
XLA Modules:
  0.0 675.8 jit_solution(17595185444159808531)
XLA Ops:
  7.2 3.9 collective-permute-start
  11.2 5.5 collective-permute-start.2
  17.3 8.4 %slice_bitcast_fusion.1 = (f32[1024,1024]{1,0:T(8,128)}, f32[1024,1024]{1,0:T(8,128)}) fusion(f32[1,2,1024,1024]{3,2,1,0:T(8,128)} %param.33), kind=kLoop, calls=%fused_computation.8 | loop fusion | bytes 16777216 | tf_op jit(solution)/shard_map/squeeze | solution.py:36
  25.8 1.3 collective-permute-start.1
  27.1 0.8 conditional.15
  27.1 0.8 broadcast_in_dim.22
  27.9 1.5 collective-permute-start.3
  29.4 5.2 fusion.6
  34.8 20.9 %collective-permute-done.1 = f32[1024,128]{1,0:T(8,128)} collective-permute-done((f32[1024,128]{1,0:T(8,128)S(1)}, f32[1024,128]{1,0:T(8,128)}, u32[]{:S(2)}, u32[]{:S(2)}) %collective-permute-start.1) | collective-permute-done | bytes 524320 | tf_op jit(solution)/shard_map/ppermute | solution.py:12
  55.7 1.4 multiply_reduce_fusion.3
  57.1 76.5 %all-reduce.1 = (f32[128]{0:T(128)S(1)}, f32[128]{0:T(128)S(1)}) all-reduce(f32[128]{0:T(128)S(1)} %get-tuple-element.115, f32[128]{0:T(128)S(1)} %get-tuple-element.114), channel_id=1, replica_groups=mesh['row'=8,'col'=16] {'row','col'}, use_global_device_ids=true, to_apply=%region_1.0 | all-reduce | flops 256 | bytes 2048 | tf_op jit(solution)/shard_map/psum | solution.py:23
  133.6 0.2 multiply_reduce_fusion.2
  133.8 62.2 %psum.44 = f32[128]{0:T(128)S(1)} all-reduce(f32[128]{0:T(128)S(1)} %get-tuple-element.118), channel_id=1, replica_groups=mesh['row'=8,'col'=16] {'row','col'}, use_global_device_ids=true, to_apply=%region_13.0 | all-reduce | flops 128 | bytes 1024 | tf_op jit(solution)/shard_map/psum | solution.py:23
  196.0 4.0 collective-permute-start.4
  200.1 4.1 collective-permute-start.6
  204.2 0.9 conditional.17
  204.2 0.8 broadcast_in_dim.25
  205.0 1.3 collective-permute-start.5
  206.3 1.3 conditional.19
  206.3 0.8 broadcast_in_dim.29
  207.6 1.3 collective-permute-start.7
  208.9 3.5 collective-permute-done.4
  212.5 9.7 %collective-permute-done.6 = f32[1024,128]{1,0:T(8,128)S(1)} collective-permute-done((f32[1024,128]{1,0:T(8,128)S(1)}, f32[1024,128]{1,0:T(8,128)S(1)}, u32[]{:S(2)}, u32[]{:S(2)}) %collective-permute-start.6) | collective-permute-done | bytes 524320 | tf_op jit(solution)/shard_map/ppermute | solution.py:12
  222.2 0.2 conditional.18
  222.4 17.7 %collective-permute-done.5 = f32[1024,128]{1,0:T(8,128)} collective-permute-done((f32[1024,128]{1,0:T(8,128)}, f32[1024,128]{1,0:T(8,128)}, u32[]{:S(2)}, u32[]{:S(2)}) %collective-permute-start.5) | collective-permute-done | bytes 524320 | tf_op jit(solution)/shard_map/ppermute | solution.py:12
  240.1 5.9 multiply_reduce_fusion.1
  246.0 74.2 %psum.45 = f32[128]{0:T(128)S(1)} all-reduce(f32[128]{0:T(128)S(1)} %get-tuple-element.123), channel_id=1, replica_groups=mesh['row'=8,'col'=16] {'row','col'}, use_global_device_ids=true, to_apply=%region_23.0 | all-reduce | flops 128 | bytes 1024 | tf_op jit(solution)/shard_map/psum | solution.py:56
  320.2 0.2 multiply_reduce_fusion
  320.3 64.6 %psum.46 = f32[128]{0:T(128)S(1)} all-reduce(f32[128]{0:T(128)S(1)} %multiply_reduce_fusion), channel_id=1, replica_groups=mesh['row'=8,'col'=16] {'row','col'}, use_global_device_ids=true, to_apply=%region_25.0 | all-reduce | flops 128 | bytes 1024 | tf_op jit(solution)/shard_map/psum | solution.py:23
  385.0 1.7 collective-permute-start.8
  386.7 3.9 collective-permute-start.10
  390.6 0.9 conditional.21
  390.6 0.8 broadcast_in_dim.33
  391.4 1.3 collective-permute-start.9
  392.7 1.0 conditional.23
  392.7 0.8 broadcast_in_dim.45
  393.7 1.3 collective-permute-start.11
  395.0 3.9 collective-permute-done.8
  399.0 10.2 %collective-permute-done.10 = f32[1024,128]{1,0:T(8,128)S(1)} collective-permute-done((f32[1024,128]{1,0:T(8,128)S(1)}, f32[1024,128]{1,0:T(8,128)S(1)}, u32[]{:S(2)}, u32[]{:S(2)}) %collective-permute-start.10) | collective-permute-done | bytes 524320 | tf_op jit(solution)/shard_map/ppermute | solution.py:12
  409.2 0.3 conditional.22
  409.5 17.4 %collective-permute-done.9 = f32[1024,128]{1,0:T(8,128)} collective-permute-done((f32[1024,128]{1,0:T(8,128)}, f32[1024,128]{1,0:T(8,128)}, u32[]{:S(2)}, u32[]{:S(2)}) %collective-permute-start.9) | collective-permute-done | bytes 524320 | tf_op jit(solution)/shard_map/ppermute | solution.py:12
  426.9 5.9 fusion.48
  432.8 75.3 %psum.47 = f32[128]{0:T(128)S(1)} all-reduce(f32[128]{0:T(128)S(1)} %fusion.48), channel_id=1, replica_groups=mesh['row'=8,'col'=16] {'row','col'}, use_global_device_ids=true, to_apply=%region_35.0 | all-reduce | flops 128 | bytes 1024 | tf_op jit(solution)/shard_map/psum | solution.py:56
  508.0 0.1 multiply_add_fusion
  508.2 9.3 %convolution_bitcast_fusion = f32[5120,128]{0,1:T(8,128)} fusion(bf16[5120,1024]{1,0:T(8,128)(2,1)} %param.35, f32[1024,128]{1,0:T(8,128)S(1)} %multiply_add_fusion), kind=kOutput, calls=%fused_computation | convolution fusion | flops 1342308352 | bytes 13631488 | tf_op jit(solution)/shard_map/dot_general | solution.py:63
  517.5 149.3 %all-reduce.4.cloned.1.call-done = f32[5120,128]{0,1:T(8,128)} async-done(((f32[5120,128]{0,1:T(8,128)}), f32[5120,128]{0,1:T(8,128)}) %all-reduce.4.cloned.1.call-update) | async-done | bytes 2621456
  666.8 1.0 constant_dynamic-slice_fusion
  667.8 0.7 copy.13
  (32 shorter events, 0.7 us)
Async XLA Ops:
  7.2 659.6 %all-reduce.4.cloned.1.call-start = ((), (), s32[]{:S(2)}) async-start(), calls=%async_computation | async-start | bytes 5242880
  7.2 27.5 %collective-permute-start = (f32[1024,128]{1,0:T(8,128)}, f32[1024,128]{1,0:T(8,128)S(1)}, u32[]{:S(2)}, u32[]{:S(2)}) collective-permute-start(f32[1024,128]{1,0:T(8,128)} %param.30), channel_id=1, source_target_pairs={{0,1},{1,2},{2,3},{3,4},{4,5},{5,6},{6,7},{7,8},{8,9},{9,10},{10,1... | collective-permute-start | bytes 1572872 | tf_op jit(solution)/shard_map/ppermute | solution.py:12
  11.2 23.6 %collective-permute-start.2 = (f32[1024,128]{1,0:T(8,128)}, f32[1024,128]{1,0:T(8,128)S(1)}, u32[]{:S(2)}, u32[]{:S(2)}) collective-permute-start(f32[1024,128]{1,0:T(8,128)} %param.30), channel_id=1, source_target_pairs={{0,2},{1,3},{2,4},{3,5},{4,6},{5,7},{6,8},{7,9},{8,10},{9,11},{10,... | collective-permute-start | bytes 1572872 | tf_op jit(solution)/shard_map/ppermute | solution.py:12
  17.3 8.4 %copy-start = (f32[1024,128]{1,0:T(8,128)S(1)}, f32[1024,128]{1,0:T(8,128)}, u32[]{:S(2)}) copy-start(f32[1024,128]{1,0:T(8,128)} %param.30) | copy-start | bytes 1572868
  25.8 3.7 copy-start.2
  25.8 30.0 %collective-permute-start.1 = (f32[1024,128]{1,0:T(8,128)S(1)}, f32[1024,128]{1,0:T(8,128)}, u32[]{:S(2)}, u32[]{:S(2)}) collective-permute-start(f32[1024,128]{1,0:T(8,128)S(1)} %get-tuple-element.126), channel_id=1, source_target_pairs={{1,0},{2,1},{3,2},{4,3},{5,4},{6,5},{7,6},{8,7},{9,8},{10,9},{11,1... | collective-permute-start | bytes 1572872 | tf_op jit(solution)/shard_map/ppermute | solution.py:12
  27.9 27.8 %collective-permute-start.3 = (f32[1024,128]{1,0:T(8,128)}, f32[1024,128]{1,0:T(8,128)}, u32[]{:S(2)}, u32[]{:S(2)}) collective-permute-start(f32[1024,128]{1,0:T(8,128)} %get-tuple-element.128), channel_id=1, source_target_pairs={{2,0},{3,1},{4,2},{5,3},{6,4},{7,5},{8,6},{9,7},{10,8},{11,9},{12,... | collective-permute-start | bytes 1572872 | tf_op jit(solution)/shard_map/ppermute | solution.py:12
  196.0 16.4 %collective-permute-start.4 = (f32[1024,128]{1,0:T(8,128)S(1)}, f32[1024,128]{1,0:T(8,128)S(1)}, u32[]{:S(2)}, u32[]{:S(2)}) collective-permute-start(f32[1024,128]{1,0:T(8,128)S(1)} %multiply_add_fusion.2), channel_id=1, source_target_pairs={{0,1},{1,2},{2,3},{3,4},{4,5},{5,6},{6,7},{7,8},{8,9},{9,10},{10,1... | collective-permute-start | bytes 1572872 | tf_op jit(solution)/shard_map/ppermute | solution.py:12
  200.1 22.1 %collective-permute-start.6 = (f32[1024,128]{1,0:T(8,128)S(1)}, f32[1024,128]{1,0:T(8,128)S(1)}, u32[]{:S(2)}, u32[]{:S(2)}) collective-permute-start(f32[1024,128]{1,0:T(8,128)S(1)} %multiply_add_fusion.2), channel_id=1, source_target_pairs={{0,2},{1,3},{2,4},{3,5},{4,6},{5,7},{6,8},{7,9},{8,10},{9,11},{10,... | collective-permute-start | bytes 1572872 | tf_op jit(solution)/shard_map/ppermute | solution.py:12
  205.0 35.0 %collective-permute-start.5 = (f32[1024,128]{1,0:T(8,128)}, f32[1024,128]{1,0:T(8,128)}, u32[]{:S(2)}, u32[]{:S(2)}) collective-permute-start(f32[1024,128]{1,0:T(8,128)} %get-tuple-element.130), channel_id=1, source_target_pairs={{1,0},{2,1},{3,2},{4,3},{5,4},{6,5},{7,6},{8,7},{9,8},{10,9},{11,1... | collective-permute-start | bytes 1572872 | tf_op jit(solution)/shard_map/ppermute | solution.py:12
  207.6 32.5 %collective-permute-start.7 = (f32[1024,128]{1,0:T(8,128)}, f32[1024,128]{1,0:T(8,128)}, u32[]{:S(2)}, u32[]{:S(2)}) collective-permute-start(f32[1024,128]{1,0:T(8,128)} %get-tuple-element.132), channel_id=1, source_target_pairs={{2,0},{3,1},{4,2},{5,3},{6,4},{7,5},{8,6},{9,7},{10,8},{11,9},{12,... | collective-permute-start | bytes 1572872 | tf_op jit(solution)/shard_map/ppermute | solution.py:12
  385.0 13.9 %collective-permute-start.8 = (f32[1024,128]{1,0:T(8,128)S(1)}, f32[1024,128]{1,0:T(8,128)S(1)}, u32[]{:S(2)}, u32[]{:S(2)}) collective-permute-start(f32[1024,128]{1,0:T(8,128)S(1)} %multiply_add_fusion.1), channel_id=1, source_target_pairs={{0,1},{1,2},{2,3},{3,4},{4,5},{5,6},{6,7},{7,8},{8,9},{9,10},{10,1... | collective-permute-start | bytes 1572872 | tf_op jit(solution)/shard_map/ppermute | solution.py:12
  386.7 22.5 %collective-permute-start.10 = (f32[1024,128]{1,0:T(8,128)S(1)}, f32[1024,128]{1,0:T(8,128)S(1)}, u32[]{:S(2)}, u32[]{:S(2)}) collective-permute-start(f32[1024,128]{1,0:T(8,128)S(1)} %multiply_add_fusion.1), channel_id=1, source_target_pairs={{0,2},{1,3},{2,4},{3,5},{4,6},{5,7},{6,8},{7,9},{8,10},{9,11},{10,... | collective-permute-start | bytes 1572872 | tf_op jit(solution)/shard_map/ppermute | solution.py:12
  391.4 35.4 %collective-permute-start.9 = (f32[1024,128]{1,0:T(8,128)}, f32[1024,128]{1,0:T(8,128)}, u32[]{:S(2)}, u32[]{:S(2)}) collective-permute-start(f32[1024,128]{1,0:T(8,128)} %get-tuple-element.134), channel_id=1, source_target_pairs={{1,0},{2,1},{3,2},{4,3},{5,4},{6,5},{7,6},{8,7},{9,8},{10,9},{11,1... | collective-permute-start | bytes 1572872 | tf_op jit(solution)/shard_map/ppermute | solution.py:12
  393.7 33.1 %collective-permute-start.11 = (f32[1024,128]{1,0:T(8,128)}, f32[1024,128]{1,0:T(8,128)}, u32[]{:S(2)}, u32[]{:S(2)}) collective-permute-start(f32[1024,128]{1,0:T(8,128)} %get-tuple-element.136), channel_id=1, source_target_pairs={{2,0},{3,1},{4,2},{5,3},{6,4},{7,5},{8,6},{9,7},{10,8},{11,9},{12,... | collective-permute-start | bytes 1572872 | tf_op jit(solution)/shard_map/ppermute | solution.py:12
  508.1 9.3 %copy-start.1 = (f32[1024,128]{1,0:T(8,128)}, f32[1024,128]{1,0:T(8,128)S(1)}, u32[]{:S(2)}) copy-start(f32[1024,128]{1,0:T(8,128)S(1)} %multiply_add_fusion) | copy-start | bytes 1572868
Sparse Core Ops, SparseCore 0:
  517.6 149.1 all-reduce.3
where the time goes:
time: 685 us; the launch traced here: 676 us
  blocking collectives  353 us (52%)
  waiting for transfers between devices  233 us (34%)
  starting transfers between devices  31.1 us (5%)
  matrix products  26.3 us (4%)
  between operations  15.4 us (2%)
  local copies, waits for them, and re-layouts  14.5 us (2%)
    psum x3, blocking collectives, squared(): return lax.psum(jnp.sum(vec * vec, axis=0), ('row', 'col'))  203 us
    psum x2, blocking collectives, body(): lax.psum(jnp.sum(direction * out, axis=0), ('row', 'col'))  149 us
    unnamed x2, waiting for transfers between devices  149 us
    ppermute x12, waiting for transfers between devices, from_behind(): return lax.ppermute(block, axis, route)  83.3 us
    ppermute x12, starting transfers between devices, from_behind(): return lax.ppermute(block, axis, route)  31 us
    dot_general x3, matrix products, body(): jnp.dot(diag_tile, apply_vec, precision=highest, preferred_element_type=j...  17 us
  transfers between devices with their start and end apart: 13, of which 8 were waited for; matrix products, arithmetic and copies ran while one was open for 3% of the time, Pallas kernels for 0%

commit v1 on v0

v1 whole, which is shorter than its diff:
```python
import functools

import jax
import jax.numpy as jnp
from jax import lax
from jax.experimental import pallas as pl
from jax.experimental.pallas import tpu as pltpu
from jax.sharding import PartitionSpec as P

MESH = pl.DeviceIdType.MESH
F32 = jnp.float32
BF16 = jnp.bfloat16
BS = 1024
K = 128
ROWS = 8
COLS = 16
CH = 256
NC = BS // CH
HALF = BS // 2
GROUP = 640
PARTS = ((0, 16, "yzx"), (16, 16, "zxy"), (32, 8, "xyz"))


def split(v):
    high = v.astype(BF16)
    return high, (v - high.astype(F32)).astype(BF16)


def both(v):
    return jnp.concatenate(split(v), axis=1)


def dot(a, b):
    return jnp.dot(a, b, preferred_element_type=F32)


def product(high, low, pair):
    wide = dot(high, pair)
    return wide[:, :K] + wide[:, K:] + dot(low, pair[:, :K])


def chunk(c):
    return pl.ds(pl.multiple_of(c * CH, CH), CH)


def kernel(
    mask, b, penalty, ld_diag, ld_low, genotypes,
    effects, scores,
    stage, tiles, flipped, geno, vec, m1, m2, pair, u2, ru2, us, rus, look, dw,
    q1, r1, d1, d2, x01, rounded, payload, ar_one, ar_two, mid,
    sc, rc, total, p0a, p0b, p0c, p1a, p1b, p1c, p2a, p2b, p2c, v0, v1, v2, w0, w1, w2,
    load_sem, geno_sem, chain_s, chain_r, ar_s, ar_r, core_s, core_r, rs_s, rs_r,
):
    row, col = lax.axis_index("row"), lax.axis_index("col")
    place = row * COLS + col
    y, core, x, z = row // 2, row % 2, col // 4, col % 4

    def hop(distance):
        to = (place + distance + ROWS * COLS) % (ROWS * COLS)
        return (to // COLS, to % COLS)

    def at(**new):
        p = dict(y=y, core=core, x=x, z=z)
        p.update(new)
        return (p["y"] * 2 + p["core"], p["x"] * 4 + p["z"])

    def load(t, h):
        n = 2 * t + h
        src = ld_diag.at[0] if t == 2 else ld_low.at[0, 1 - t]
        return pltpu.make_async_copy(
            src.at[pl.ds(h * HALF, HALF)], stage.at[n % 2], load_sem.at[n % 2]
        )

    load(0, 0).start()
    load(0, 1).start()
    geno_copy = pltpu.make_async_copy(genotypes, geno, geno_sem)

    barrier = pltpu.get_barrier_semaphore()
    for distance in (1, 2, -1, -2):
        pl.semaphore_signal(barrier, inc=1, device_id=hop(distance), device_id_type=MESH)

    @pl.loop(1, COLS)
    def _(k):
        pl.semaphore_signal(barrier, inc=1, device_id=(row, (col + k) % COLS), device_id_type=MESH)

    @pl.loop(1, ROWS)
    def _(k):
        pl.semaphore_signal(barrier, inc=1, device_id=((row + k) % ROWS, col), device_id_type=MESH)

    pl.semaphore_wait(barrier, 4 + COLS - 1 + ROWS - 1)

    def remote(src, dst, send, recv, device):
        return pltpu.make_async_remote_copy(
            src_ref=src, dst_ref=dst, send_sem=send, recv_sem=recv,
            device_id=device, device_id_type=MESH,
        )

    def source(e):
        return b if e == 0 else vec.at[e - 1]

    def send_own(e, c):
        return remote(source(e).at[chunk(c)], m1.at[e, chunk(c)],
                      chain_s.at[e, 0, c], chain_r.at[e, 0, c], hop(1))

    def send_on(e, c):
        return remote(m1.at[e, chunk(c)], m2.at[e, chunk(c)],
                      chain_s.at[e, 1, c], chain_r.at[e, 1, c], hop(1))

    def send_u2(e, c):
        return remote(u2.at[e, chunk(c)], ru2.at[e, chunk(c)],
                      chain_s.at[e, 2, c], chain_r.at[e, 2, c], hop(-1))

    def send_us(e, c):
        return remote(us.at[e, chunk(c)], rus.at[e, chunk(c)],
                      chain_s.at[e, 3, c], chain_r.at[e, 3, c], hop(-1))

    @pl.loop(0, NC)
    def _(c):
        send_own(0, c).start()

    def convert(t):
        for h in range(2):
            load(t, h).wait()
            n = 2 * t + h

            @pl.loop(0, HALF // CH)
            def _(c):
                block = stage[n % 2, chunk(c), :]
                if t < 2:
                    block = block * mask[1 - t]
                rows = pl.ds(pl.multiple_of(h * HALF + c * CH, CH), CH)
                high, low = split(block)
                tiles[t, 0, rows, :] = high
                tiles[t, 1, rows, :] = low
                if t < 2:
                    high, low = split(block.T)
                    flipped[t, 0, :, rows] = high
                    flipped[t, 1, :, rows] = low

            if t < 2:
                load(t + 1, h).start()

    def ar_col(n, k):
        return remote(payload.at[n], ar_one.at[n, k], ar_s.at[n, 0, k], ar_r.at[n, 0, k],
                      (row, (col + k) % COLS))

    def ar_row(n, k):
        return remote(mid.at[n], ar_two.at[n, k], ar_s.at[n, 1, k], ar_r.at[n, 1, k],
                      ((row + k) % ROWS, col))

    def ar_start(n, rows):
        for j in range(8):
            payload[n, j : j + 1, :] = rows[j] if j < len(rows) else jnp.zeros((1, K), F32)

        @pl.loop(1, COLS)
        def _(k):
            ar_col(n, k).start()

    def ar_middle(n):
        @pl.loop(1, COLS)
        def _(k):
            ar_col(n, k).wait_recv()

        acc = payload[n]
        for k in range(1, COLS):
            acc = acc + ar_one[n, k]
        mid[n] = acc

        @pl.loop(1, ROWS)
        def _(k):
            ar_row(n, k).start()

    def ar_end(n):
        @pl.loop(1, ROWS)
        def _(k):
            ar_row(n, k).wait_recv()

        acc = mid[n]
        for k in range(1, ROWS):
            acc = acc + ar_two[n, k]
        return acc

    def column(v):
        return jnp.sum(v, axis=0, keepdims=True)

    def over_chunks(body, count):
        zero = jnp.zeros((1, K), F32)
        return lax.fori_loop(0, NC, body, (zero,) * count)

    def exchange(e, last, early, late):
        src = source(e)

        @pl.loop(0, NC)
        def _(c):
            pair[chunk(c), :] = both(src[chunk(c), :])

        early()
        if e == 0:
            convert(0)
        if not last:
            @pl.loop(0, NC)
            def _(c):
                u2[e, chunk(c), :] = product(flipped[0, 0, chunk(c), :], flipped[0, 1, chunk(c), :], pair[...])
                send_u2(e, c).start()

        if e == 0:
            convert(1)

        @pl.loop(0, NC)
        def _(c):
            send_own(e, c).wait_recv()
            send_on(e, c).start()
            there = both(m1[e, chunk(c), :])
            for r in range(NC):
                rows = pl.ds(r * CH, CH)
                part = product(tiles[1, 0, rows, chunk(c)], tiles[1, 1, rows, chunk(c)], there)
                part = jnp.where(c == 0, part, part + look[e, rows, :])
                look[e, rows, :] = part
            if not last:
                up = product(flipped[1, 0, chunk(c), :], flipped[1, 1, chunk(c), :], pair[...])
                send_u2(e, c).wait_recv()
                us[e, chunk(c), :] = up + ru2[e, chunk(c), :]
                send_us(e, c).start()

        if e == 0:
            convert(2)

        @pl.loop(0, NC)
        def _(c):
            dw[chunk(c), :] = (
                product(tiles[2, 0, chunk(c), :], tiles[2, 1, chunk(c), :], pair[...])
                + penalty[...] * src[chunk(c), :]
            )

        late()

        @pl.loop(0, NC)
        def _(c):
            send_on(e, c).wait_recv()
            there = both(m2[e, chunk(c), :])
            for r in range(NC):
                rows = pl.ds(r * CH, CH)
                look[e, rows, :] += product(tiles[0, 0, rows, chunk(c)], tiles[0, 1, rows, chunk(c)], there)

    def finish(e, c):
        down = look[e, chunk(c), :]
        mine = dw[chunk(c), :]
        send_us(e, c).wait_recv()
        out = mine + down + rus[e, chunk(c), :]
        look[e, chunk(c), :] = mine + 2.0 * down
        vec[e, chunk(c), :] = out
        send_own(e + 1, c).start()
        return out

    exchange(0, False, lambda: None, lambda: None)
    geno_copy.start()

    def one(c, sums):
        out = finish(0, c)
        here = b[chunk(c), :]
        return (sums[0] + column(here * here), sums[1] + column(here * out), sums[2] + column(out * out))

    sums_one = over_chunks(one, 3)

    coef = {}

    def solve_one():
        got = ar_end(0)
        bb, bq, qq = got[0:1], got[1:2], got[2:3]
        alpha = bb / bq
        after = jnp.maximum(bb - 2.0 * alpha * bq + alpha * alpha * qq, 0.0)
        coef["a0"], coef["b1"] = alpha, after / bb

    def early_one():
        ar_start(0, sums_one)

    def late_one():
        ar_middle(0)
        solve_one()

    exchange(1, False, early_one, late_one)
    a0, b1 = coef["a0"], coef["b1"]

    def two(c, sums):
        s = finish(1, c)
        here, q = b[chunk(c), :], vec[0, chunk(c), :]
        res = here - a0 * q
        direction = res + b1 * here
        image = (1.0 + b1) * q - a0 * s
        r1[chunk(c), :] = res
        d1[chunk(c), :] = direction
        q1[chunk(c), :] = image
        terms = (res * res, res * direction, direction * image, res * image, image * image)
        return tuple(t + column(v) for t, v in zip(sums, terms))

    sums_two = over_chunks(two, 5)

    def early_two():
        ar_start(1, sums_two)

    def late_two():
        ar_middle(1)
        got = ar_end(1)
        rr, rd, dq, rq, qq = (got[j : j + 1] for j in range(5))
        alpha = rd / dq
        after = jnp.maximum(rr - 2.0 * alpha * rq + alpha * alpha * qq, 0.0)
        beta = after / rr
        coef["a1"], coef["b2"] = alpha, beta

        def body(c, sums):
            res = r1[chunk(c), :] - alpha * q1[chunk(c), :]
            direction = res + beta * d1[chunk(c), :]
            d2[chunk(c), :] = direction
            x01[chunk(c), :] = a0 * b[chunk(c), :] + alpha * d1[chunk(c), :]
            return (sums[0] + column(res * direction),)

        coef["rd2"] = over_chunks(body, 1)[0]

    exchange(2, True, early_two, late_two)
    a1, b2 = coef["a1"], coef["b2"]
    c0 = 1.0 + b2 * (1.0 + b1)
    c1 = -a0 - a1 * (1.0 + b1) - b2 * a0
    c2 = a1 * a0

    def three(c, sums):
        third = dw[chunk(c), :] + 2.0 * look[2, chunk(c), :]
        image = c0 * look[0, chunk(c), :] + c1 * look[1, chunk(c), :] + c2 * third
        return (sums[0] + column(d2[chunk(c), :] * image),)

    dq2 = over_chunks(three, 1)[0]
    ar_start(2, (coef["rd2"], dq2))
    geno_copy.wait()
    ar_middle(2)
    got = ar_end(2)
    a2 = got[0:1] / got[1:2]

    @pl.loop(0, NC)
    def _(c):
        value = x01[chunk(c), :] + a2 * d2[chunk(c), :]
        effects[chunk(c), :] = value
        rounded[chunk(c), :] = value.astype(BF16)

    def people(j, which):
        rows = pl.ds(pl.multiple_of((j * 2 + which) * GROUP, GROUP), GROUP)
        return dot(geno[rows, :], rounded[...]).reshape(4, 4, 40, K)

    def core_copy(j):
        return remote(sc.at[j], rc.at[j], core_s.at[j], core_r.at[j], at(core=1 - core))

    @pl.loop(0, 4)
    def _(j):
        sc[j] = people(j, 1 - core)
        core_copy(j).start()

    @pl.loop(0, 4)
    def _(j):
        mine = people(j, core)
        core_copy(j).wait_recv()
        total[j] = mine + rc[j]

    def axis_copy(step, part, k):
        start, size, order = PARTS[part]
        axis = order[step]
        mine = dict(y=y, x=x, z=z)[axis]
        to = (mine + k) % 4
        dst = ((p0a, p0b, p0c), (p1a, p1b, p1c), (p2a, p2b, p2c))[part][step].at[k - 1]
        if step == 0:
            rows = pl.ds(start, size)
            src = {"y": lambda: total.at[to, :, :, rows, :],
                   "x": lambda: total.at[:, to, :, rows, :],
                   "z": lambda: total.at[:, :, to, rows, :]}[axis]()
        elif step == 1:
            left = [a for a in "yxz" if a != order[0]]
            ref = (v0, v1, v2)[part]
            src = ref.at[to] if left[0] == axis else ref.at[:, to]
        else:
            src = (w0, w1, w2)[part].at[to]
        return remote(src, dst, rs_s.at[step, part, k], rs_r.at[step, part, k], at(**{axis: to}))

    for step in range(3):
        for k in (1, 3, 2):
            for part in range(3):
                axis_copy(step, part, k).start()
        for part in range(3):
            start, size, order = PARTS[part]
            axis = order[step]
            mine = dict(y=y, x=x, z=z)[axis]
            rows = pl.ds(start, size)
            if step == 0:
                acc = {"y": lambda: total[mine, :, :, rows, :],
                       "x": lambda: total[:, mine, :, rows, :],
                       "z": lambda: total[:, :, mine, rows, :]}[axis]()
            elif step == 1:
                left = [a for a in "yxz" if a != order[0]]
                ref = (v0, v1, v2)[part]
                acc = ref[mine] if left[0] == axis else ref[:, mine]
            else:
                acc = (w0, w1, w2)[part][mine]
            got = ((p0a, p0b, p0c), (p1a, p1b, p1c), (p2a, p2b, p2c))[part][step]
            for k in (1, 3, 2):
                axis_copy(step, part, k).wait_recv()
                acc = acc + got[k - 1]
            if step == 0:
                (v0, v1, v2)[part][...] = acc
            elif step == 1:
                (w0, w1, w2)[part][...] = acc
            else:
                scores[rows, :] = acc

    for e in range(3):
        @pl.loop(0, NC)
        def _(c):
            send_own(e, c).wait_send()
            send_on(e, c).wait_send()
            if e < 2:
                send_u2(e, c).wait_send()
                send_us(e, c).wait_send()

        @pl.loop(1, COLS)
        def _(k):
            ar_col(e, k).wait_send()

        @pl.loop(1, ROWS)
        def _(k):
            ar_row(e, k).wait_send()

    @pl.loop(0, 4)
    def _(j):
        core_copy(j).wait_send()

    for step in range(3):
        for part in range(3):
            for k in (1, 2, 3):
                axis_copy(step, part, k).wait_send()


def body(marginal, penalty, ld_diag, ld_low, band, genotypes):
    place = lax.axis_index(("row", "col"))
    reach = jnp.arange(1, 3)
    mask = jnp.logical_and(band[0] >= reach, place >= reach).astype(F32)
    vmem = pl.BlockSpec(memory_space=pltpu.VMEM)
    smem = pl.BlockSpec(memory_space=pltpu.SMEM)
    hbm = pl.BlockSpec(memory_space=pl.ANY)
    big = lambda *lead: pltpu.VMEM((*lead, BS, K), F32)
    parts = []
    for _, size, order in PARTS:
        parts += [pltpu.VMEM((3, 4, 4, size, K), F32), pltpu.VMEM((3, 4, size, K), F32), pltpu.VMEM((3, size, K), F32)]
    dma = pltpu.SemaphoreType.DMA
    return pl.pallas_call(
        kernel,
        out_shape=(jax.ShapeDtypeStruct((BS, K), F32), jax.ShapeDtypeStruct((40, K), F32)),
        in_specs=[smem, vmem, vmem, hbm, hbm, hbm],
        out_specs=(vmem, vmem),
        scratch_shapes=[
            pltpu.VMEM((2, HALF, BS), F32),
            pltpu.VMEM((3, 2, BS, BS), BF16),
            pltpu.VMEM((2, 2, BS, BS), BF16),
            pltpu.VMEM((8 * GROUP, BS), BF16),
            big(2), big(3), big(3),
            pltpu.VMEM((BS, 2 * K), BF16),
            big(2), big(2), big(2), big(2), big(3), big(),
            big(), big(), big(), big(), big(),
            pltpu.VMEM((BS, K), BF16),
            pltpu.VMEM((3, 8, K), F32),
            pltpu.VMEM((3, COLS, 8, K), F32),
            pltpu.VMEM((3, ROWS, 8, K), F32),
            pltpu.VMEM((3, 8, K), F32),
            pltpu.VMEM((4, 4, 4, 40, K), F32),
            pltpu.VMEM((4, 4, 4, 40, K), F32),
            pltpu.VMEM((4, 4, 4, 40, K), F32),
            *parts,
            *[pltpu.VMEM((4, 4, size, K), F32) for _, size, _ in PARTS],
            *[pltpu.VMEM((4, size, K), F32) for _, size, _ in PARTS],
            dma((2,)), dma,
            dma((3, 4, NC)), dma((3, 4, NC)),
            dma((3, 2, COLS)), dma((3, 2, COLS)),
            dma((4,)), dma((4,)),
            dma((3, 3, 4)), dma((3, 3, 4)),
        ],
        compiler_params=pltpu.CompilerParams(
            collective_id=0, has_side_effects=True, vmem_limit_bytes=62 * 1024 * 1024
        ),
    )(mask, marginal, penalty.reshape(1, K), ld_diag, ld_low, genotypes)


def solution(mesh):
    placed = (
        P(("row", "col"), None),
        P(),
        P(("row", "col"), None, None),
        P(("row", "col"), None, None, None),
        P(("row", "col")),
        P(None, ("row", "col")),
    )
    return jax.shard_map(
        body,
        mesh=mesh,
        in_specs=placed,
        out_specs=(P(("row", "col"), None), P(("row", "col"), None)),
        check_vma=False,
    )
```

time: 685 us -> 126 us (0.18); the launches traced: 676 us -> 125 us
  blocking collectives: 353 us -> 0 us
  waiting for transfers between devices: 233 us -> 0 us
  Pallas kernels: 0 us -> 120 us
  starting transfers between devices: 31.1 us -> 0 us
  matrix products: 26.3 us -> 0 us
  between operations: 15.4 us -> 1.29 us
  local copies, waits for them, and re-layouts: 14.5 us -> 3.2 us
    psum x5 -> x0, blocking collectives: 353 us -> none  [the longest x3 203 us: squared(): return lax.psum(jnp.sum(vec * vec, axis=0), ('row', 'col'))]
    unnamed x2 -> x0, waiting for transfers between devices: 149 us -> none
    pallas_call x0 -> x1, Pallas kernels: none -> 120 us  [body(): pl.pallas_call(kernel, out_shape=(jax.ShapeDtypeStruct((BS, K), F32), jax...]
    ppermute x12 -> x0, waiting for transfers between devices: 83.3 us -> none  [from_behind(): return lax.ppermute(block, axis, route)]
    ppermute x12 -> x0, starting transfers between devices: 31 us -> none  [from_behind(): return lax.ppermute(block, axis, route)]
    dot_general x4 -> x0, matrix products: 26.3 us -> none  [the longest x3 17 us: body(): jnp.dot(diag_tile, apply_vec, precision=highest, preferred_element_type=j...]
    squeeze x1 -> x0, local copies, waits for them, and re-layouts: 8.39 us -> none  [body(): tile = ld_low[0, dist - 1]]
  transfers between devices with their start and end apart: 13 -> 0, of which waited for: 8 -> 0; matrix products, arithmetic and copies ran while one was open for 3% -> 0% of each run, Pallas kernels for 0% -> 0%
where the time goes in v1:
time: 126 us; the launch traced here: 125 us
  Pallas kernels  120 us (95%)
  local copies, waits for them, and re-layouts  3.2 us (3%)
  between operations  1.29 us (1%)
    pallas_call x1, Pallas kernels, body(): pl.pallas_call(kernel, out_shape=(jax.ShapeDtypeStruct((BS, K), F32), jax...  120 us
    unnamed x2, local copies, waits for them, and re-layouts  3.2 us

profile of v1, /device:TPU:0, one launch (start us, length us, event | category | flops | bytes accessed | tf_op | source)
XLA Modules:
  0.0 125.3 jit_solution(3776353331523743190)
XLA Ops:
  1.3 0.5 and_convert_fusion.mask
  1.8 120.3 %shard_map.77 = (f32[1024,128]{1,0:T(8,128)}, f32[40,128]{1,0:T(8,128)}) custom-call(f32[2]{0:T(128)} %and_convert_fusion.mask, f32[1024,128]{1,0:T(8,128)} %b.1, f32[1,128]{1,0:T(1,128)} %bitcast.3, f32[1,1024,1024]{2,1,0:T(8,128)} %ld_diag.1, f32[1,2,1024,1024]{3,2,1,0:T(8,128)} %ld_low.1, bf16[5120,1024]{1,0:T(8,128)(2,1)} %genotypes.1), custom_call_target="tpu_custom_call" | custom-call | tf_op jit(solution)/shard_map/pallas_call | solution.py:449
  122.1 1.9 %copy.11 = f32[1024,128]{1,0:T(8,128)} copy(f32[1024,128]{1,0:T(8,128)} %get-tuple-element.4) | data formatting | bytes 1048576
  124.0 1.3 %copy.12 = f32[40,128]{1,0:T(8,128)} copy(f32[40,128]{1,0:T(8,128)} %get-tuple-element.5) | data formatting | bytes 40960

commit v2 on v1

v2 whole, which is shorter than its diff:
```python
import jax
import jax.numpy as jnp
from jax import lax
from jax.experimental import pallas as pl
from jax.experimental.pallas import tpu as pltpu
from jax.sharding import PartitionSpec as P

MESH = pl.DeviceIdType.MESH
F32 = jnp.float32
BF16 = jnp.bfloat16
BS = 1024
K = 128
ROWS = 8
COLS = 16
CH = 256
NC = BS // CH
GROUP = 640
PARTS = ((0, 16, "yzx"), (16, 16, "zxy"), (32, 8, "xyz"))


def split(v):
    high = v.astype(BF16)
    return high, (v - high.astype(F32)).astype(BF16)


def both(v):
    return jnp.concatenate(split(v), axis=1)


def dot(a, b):
    return jnp.dot(a, b, preferred_element_type=F32)


def product(high, low, pair):
    wide = dot(high, pair)
    return wide[:, :K] + wide[:, K:] + dot(low, pair[:, :K])


def chunk(c):
    return pl.ds(pl.multiple_of(c * CH, CH), CH)


def kernel(
    band, marginal, penalty_in, ld_diag, ld_low, genotypes,
    effects, scores,
    stage, diag_stage, tiles, flipped, geno, vec, m1, m2, via, pair, tail, u2, ru2, us, rus, look, dw,
    penalty, q1, r1, d1, d2, x01, rounded, payload, ar_one, ar_two, mid,
    sc, rc, total, p0a, p0b, p0c, p1a, p1b, p1c, p2a, p2b, p2c, v0, v1, v2, w0, w1, w2, mine40,
    small_sem, load_sem, diag_sem, geno_sem, out_sem, chain_s, chain_r, ar_s, ar_r, core_s, core_r,
    rs_s, rs_r, first_s, first_r,
):
    row, col = lax.axis_index("row"), lax.axis_index("col")
    place = row * COLS + col
    y, core, x, z = row // 2, row % 2, col // 4, col % 4

    def hop(distance):
        to = (place + distance + ROWS * COLS) % (ROWS * COLS)
        return (to // COLS, to % COLS)

    def at(**new):
        p = dict(y=y, core=core, x=x, z=z)
        p.update(new)
        return (p["y"] * 2 + p["core"], p["x"] * 4 + p["z"])

    back = at(z=(z + 3) % 4)
    onward = hop(jnp.where(z == 3, -1, 3))
    from_onward = hop(jnp.where(z == 2, 1, -3))

    b_copy = pltpu.make_async_copy(marginal, vec.at[0], small_sem.at[0])
    penalty_copy = pltpu.make_async_copy(penalty_in, penalty, small_sem.at[1])
    geno_copy = pltpu.make_async_copy(genotypes, geno, geno_sem)

    def load(t, c):
        return pltpu.make_async_copy(ld_low.at[0, 1 - t, :, chunk(c)], stage.at[c], load_sem.at[c])

    def load_diag(c):
        return pltpu.make_async_copy(ld_diag.at[0, chunk(c)], diag_stage.at[c], diag_sem.at[c])

    b_copy.start()
    penalty_copy.start()
    for c in range(NC):
        load(0, c).start()

    barrier = pltpu.get_barrier_semaphore()
    for device in (hop(1), hop(2), hop(-1), hop(-2), onward, from_onward):
        pl.semaphore_signal(barrier, inc=1, device_id=device, device_id_type=MESH)

    @pl.loop(1, COLS)
    def _(k):
        pl.semaphore_signal(barrier, inc=1, device_id=(row, (col + k) % COLS), device_id_type=MESH)

    @pl.loop(1, ROWS)
    def _(k):
        pl.semaphore_signal(barrier, inc=1, device_id=((row + k) % ROWS, col), device_id_type=MESH)

    b_copy.wait()
    pl.semaphore_wait(barrier, 6 + COLS - 1 + ROWS - 1)

    def remote(src, dst, send, recv, device):
        return pltpu.make_async_remote_copy(
            src_ref=src, dst_ref=dst, send_sem=send, recv_sem=recv,
            device_id=device, device_id_type=MESH,
        )

    def send_own(e, c):
        return remote(vec.at[e, chunk(c)], m1.at[e, chunk(c)],
                      chain_s.at[e, 0, c], chain_r.at[e, 0, c], hop(1))

    def send_on(e, c):
        return remote(m1.at[e, chunk(c)], m2.at[e, chunk(c)],
                      chain_s.at[e, 1, c], chain_r.at[e, 1, c], hop(1))

    def send_u2(e, c):
        return remote(u2.at[e, chunk(c)], ru2.at[e, chunk(c)],
                      chain_s.at[e, 2, c], chain_r.at[e, 2, c], hop(-1))

    def send_us(e, c):
        return remote(us.at[e, chunk(c)], rus.at[e, chunk(c)],
                      chain_s.at[e, 3, c], chain_r.at[e, 3, c], hop(-1))

    def send_back(c):
        return remote(vec.at[2, chunk(c)], via.at[chunk(c)],
                      chain_s.at[2, 2, c], chain_r.at[2, 2, c], back)

    def send_onward(c):
        return remote(via.at[chunk(c)], m2.at[2, chunk(c)],
                      chain_s.at[2, 3, c], chain_r.at[2, 3, c], onward)

    @pl.loop(0, NC)
    def _(c):
        send_own(0, c).start()

    for c in range(NC):
        load_diag(c).start()

    place_f = [place >= distance for distance in (1, 2)]
    active = [
        jnp.where(jnp.logical_and(place_f[d - 1], band[0] >= d), 1.0, 0.0).astype(F32) for d in (1, 2)
    ]

    def convert(t, c):
        load(t, c).wait()
        block = stage[c] * active[1 - t]
        high, low = split(block)
        tiles[t, 0, :, chunk(c)] = high
        tiles[t, 1, :, chunk(c)] = low
        high, low = split(block.T)
        flipped[t, 0, chunk(c), :] = high
        flipped[t, 1, chunk(c), :] = low
        if t == 0:
            load(1, c).start()

    def ar_col(n, k):
        return remote(payload.at[n], ar_one.at[n, k], ar_s.at[n, 0, k], ar_r.at[n, 0, k],
                      (row, (col + k) % COLS))

    def ar_row(n, k):
        return remote(mid.at[n], ar_two.at[n, k], ar_s.at[n, 1, k], ar_r.at[n, 1, k],
                      ((row + k) % ROWS, col))

    def ar_start(n, rows):
        for j in range(8):
            payload[n, j : j + 1, :] = rows[j] if j < len(rows) else jnp.zeros((1, K), F32)

        @pl.loop(1, COLS)
        def _(k):
            ar_col(n, k).start()

    def ar_middle(n):
        @pl.loop(1, COLS)
        def _(k):
            ar_col(n, k).wait_recv()

        acc = payload[n]
        for k in range(1, COLS):
            acc = acc + ar_one[n, k]
        mid[n] = acc

        @pl.loop(1, ROWS)
        def _(k):
            ar_row(n, k).start()

    def ar_end(n):
        @pl.loop(1, ROWS)
        def _(k):
            ar_row(n, k).wait_recv()

        acc = mid[n]
        for k in range(1, ROWS):
            acc = acc + ar_two[n, k]
        return acc

    def column(v):
        return jnp.sum(v, axis=0, keepdims=True)

    def over_chunks(body, count):
        zero = jnp.zeros((1, K), F32)
        return lax.fori_loop(0, NC, body, (zero,) * count)

    def add_second(e, c):
        there = both(m2[e, chunk(c), :])
        for r in range(NC):
            rows = pl.ds(r * CH, CH)
            look[e, rows, :] += product(tiles[0, 0, rows, chunk(c)], tiles[0, 1, rows, chunk(c)], there)

    def add_first(e, c):
        there = both(m1[e, chunk(c), :])
        for r in range(NC):
            rows = pl.ds(r * CH, CH)
            part = product(tiles[1, 0, rows, chunk(c)], tiles[1, 1, rows, chunk(c)], there)
            look[e, rows, :] = jnp.where(c == 0, part, part + look[e, rows, :])

    def below(e, r, last):
        return look[e, chunk(r), :] + product(
            tiles[0, 0, chunk(r), chunk(last)], tiles[0, 1, chunk(r), chunk(last)], tail[...]
        )

    def diagonal(e):
        @pl.loop(0, NC)
        def _(c):
            if e == 0:
                load_diag(c).wait()
                high, low = split(diag_stage[c])
                tiles[2, 0, chunk(c), :] = high
                tiles[2, 1, chunk(c), :] = low
            dw[chunk(c), :] = (
                product(tiles[2, 0, chunk(c), :], tiles[2, 1, chunk(c), :], pair[...])
                + penalty[...] * vec[e, chunk(c), :]
            )

    def exchange(e, early, middle, late):
        @pl.loop(0, NC)
        def _(c):
            if e == 0:
                convert(0, c)
            u2[e, chunk(c), :] = product(flipped[0, 0, chunk(c), :], flipped[0, 1, chunk(c), :], pair[...])
            send_u2(e, c).start()

        early()

        @pl.loop(0, NC)
        def _(c):
            send_own(e, c).wait_recv()
            send_on(e, c).start()
            if e == 0:
                convert(1, c)
            up = product(flipped[1, 0, chunk(c), :], flipped[1, 1, chunk(c), :], pair[...])
            send_u2(e, c).wait_recv()
            us[e, chunk(c), :] = up + ru2[e, chunk(c), :]
            send_us(e, c).start()
            add_first(e, c)

        middle()
        diagonal(e)
        late()

        @pl.loop(0, NC - 1)
        def _(c):
            send_on(e, c).wait_recv()
            add_second(e, c)

        send_on(e, NC - 1).wait_recv()
        tail[...] = both(m2[e, chunk(NC - 1), :])

    def finish(e, c):
        down = below(e, c, NC - 1)
        part = dw[chunk(c), :]
        send_us(e, c).wait_recv()
        out = part + down + rus[e, chunk(c), :]
        vec[e + 1, chunk(c), :] = out
        send_own(e + 1, c).start()
        look[e, chunk(c), :] = part + 2.0 * down
        pair[chunk(c), :] = both(out)
        return out

    @pl.loop(0, NC)
    def _(c):
        pair[chunk(c), :] = both(vec[0, chunk(c), :])

    penalty_copy.wait()
    exchange(0, lambda: None, geno_copy.start, lambda: None)

    def one(c, sums):
        out = finish(0, c)
        here = vec[0, chunk(c), :]
        return (sums[0] + column(here * here), sums[1] + column(here * out), sums[2] + column(out * out))

    sums_one = over_chunks(one, 3)

    coef = {}

    def late_one():
        got = ar_end(0)
        bb, bq, qq = got[0:1], got[1:2], got[2:3]
        alpha = bb / bq
        after = jnp.maximum(bb - 2.0 * alpha * bq + alpha * alpha * qq, 0.0)
        coef["a0"], coef["b1"] = alpha, after / bb

    exchange(1, lambda: ar_start(0, sums_one), lambda: ar_middle(0), late_one)
    a0, b1 = coef["a0"], coef["b1"]

    def two(c, sums):
        s = finish(1, c)
        here, q = vec[0, chunk(c), :], vec[1, chunk(c), :]
        res = here - a0 * q
        direction = res + b1 * here
        image = (1.0 + b1) * q - a0 * s
        r1[chunk(c), :] = res
        d1[chunk(c), :] = direction
        q1[chunk(c), :] = image
        terms = (res * res, res * direction, direction * image, res * image, image * image)
        return tuple(t + column(v) for t, v in zip(sums, terms))

    sums_two = over_chunks(two, 5)
    for c in (2, 3):
        send_back(c).start()
    ar_start(1, sums_two)

    for c in range(NC):
        send_own(2, c).wait_recv()
        if c < 2:
            send_on(2, c).start()
        else:
            send_back(c).wait_recv()
            send_onward(c).start()
        add_first(2, c)
    ar_middle(1)
    diagonal(2)
    got = ar_end(1)
    rr, rd, dq, rq, qq = (got[j : j + 1] for j in range(5))
    a1 = rd / dq
    after = jnp.maximum(rr - 2.0 * a1 * rq + a1 * a1 * qq, 0.0)
    b2 = after / rr

    def update(c, sums):
        res = r1[chunk(c), :] - a1 * q1[chunk(c), :]
        direction = res + b2 * d1[chunk(c), :]
        d2[chunk(c), :] = direction
        x01[chunk(c), :] = a0 * vec[0, chunk(c), :] + a1 * d1[chunk(c), :]
        return (sums[0] + column(res * direction),)

    rd2 = over_chunks(update, 1)[0]
    c0 = 1.0 + b2 * (1.0 + b1)
    c1 = -a0 - a1 * (1.0 + b1) - b2 * a0
    c2 = a1 * a0

    for c in (2, 3):
        send_onward(c).wait_recv()
        add_second(2, c)
    send_on(2, 0).wait_recv()
    add_second(2, 0)
    send_on(2, 1).wait_recv()
    tail[...] = both(m2[2, chunk(1), :])

    def three(c, sums):
        third = dw[chunk(c), :] + 2.0 * below(2, c, 1)
        image = c0 * look[0, chunk(c), :] + c1 * look[1, chunk(c), :] + c2 * third
        return (sums[0] + column(d2[chunk(c), :] * image),)

    dq2 = over_chunks(three, 1)[0]
    ar_start(2, (rd2, dq2))
    geno_copy.wait()
    ar_middle(2)
    got = ar_end(2)
    a2 = got[0:1] / got[1:2]

    @pl.loop(0, NC)
    def _(c):
        value = x01[chunk(c), :] + a2 * d2[chunk(c), :]
        x01[chunk(c), :] = value
        rounded[chunk(c), :] = value.astype(BF16)

    effects_copy = pltpu.make_async_copy(x01, effects, out_sem.at[0])
    effects_copy.start()

    def people(j, which):
        rows = pl.ds(pl.multiple_of((j * 2 + which) * GROUP, GROUP), GROUP)
        return dot(geno[rows, :], rounded[...]).reshape(4, 4, 40, K)

    def core_copy(j):
        return remote(sc.at[j], rc.at[j], core_s.at[j], core_r.at[j], at(core=1 - core))

    def rows_of(part):
        return pl.ds(PARTS[part][0], PARTS[part][1])

    def first_y(k):
        to = (y + k) % 4
        return remote(total.at[to, :, :, rows_of(0), :], p0a.at[k - 1], rs_s.at[0, 0, k], rs_r.at[0, 0, k], at(y=to))

    def first_z(j, k):
        to = (z + k) % 4
        return remote(total.at[j, :, to, rows_of(1), :], p1a.at[k - 1, j], first_s.at[0, k, j], first_r.at[0, k, j], at(z=to))

    def first_x(j, k):
        to = (x + k) % 4
        return remote(total.at[j, to, :, rows_of(2), :], p2a.at[k - 1, j], first_s.at[1, k, j], first_r.at[1, k, j], at(x=to))

    def other_core(n):
        j = (y + n) % 4
        sc[j] = people(j, 1 - core)
        core_copy(j).start()

    def own_core(n):
        j = (y + n) % 4
        mine = people(j, core)
        core_copy(j).wait_recv()
        total[j] = mine + rc[j]
        if n > 0:
            first_y(n).start()
        for k in (1, 3, 2):
            first_z(j, k).start()
            first_x(j, k).start()

    other_core(1)
    other_core(3)
    own_core(1)
    other_core(2)
    own_core(3)
    other_core(0)
    own_core(2)
    own_core(0)

    landed = ((p0a, p0b, p0c), (p1a, p1b, p1c), (p2a, p2b, p2c))
    halfway = ((v0, w0), (v1, w1), (v2, w2))

    def axis_copy(step, part, k):
        order = PARTS[part][2]
        axis = order[step]
        to = (dict(y=y, x=x, z=z)[axis] + k) % 4
        ref = halfway[part][step - 1]
        left = [a for a in "yxz" if a != order[0]]
        src = ref.at[:, to] if step == 1 and left[1] == axis else ref.at[to]
        return remote(src, landed[part][step].at[k - 1], rs_s.at[step, part, k], rs_r.at[step, part, k], at(**{axis: to}))

    def send_axis(step, part):
        for k in (1, 3, 2):
            axis_copy(step, part, k).start()

    for part in (2, 0, 1):
        acc = (
            lambda: total[y, :, :, rows_of(0), :],
            lambda: total[:, :, z, rows_of(1), :],
            lambda: total[:, x, :, rows_of(2), :],
        )[part]()
        for k in (1, 3, 2):
            if part == 0:
                first_y(k).wait_recv()
            else:
                for n in (1, 3, 2, 0):
                    (first_z, first_x)[part - 1]((y + n) % 4, k).wait_recv()
            acc = acc + landed[part][0][k - 1]
        halfway[part][0][...] = acc
        send_axis(1, part)
    for step in (1, 2):
        for part in (2, 0, 1):
            order = PARTS[part][2]
            axis = order[step]
            mine = dict(y=y, x=x, z=z)[axis]
            ref = halfway[part][step - 1]
            left = [a for a in "yxz" if a != order[0]]
            acc = ref[:, mine] if step == 1 and left[1] == axis else ref[mine]
            for k in (1, 3, 2):
                axis_copy(step, part, k).wait_recv()
                acc = acc + landed[part][step][k - 1]
            if step == 1:
                halfway[part][1][...] = acc
                send_axis(2, part)
            else:
                mine40[rows_of(part), :] = acc

    scores_copy = pltpu.make_async_copy(mine40, scores, out_sem.at[1])
    scores_copy.start()

    for e in range(3):
        @pl.loop(0, NC)
        def _(c):
            send_own(e, c).wait_send()
            if e < 2:
                send_on(e, c).wait_send()
                send_u2(e, c).wait_send()
                send_us(e, c).wait_send()

        @pl.loop(1, COLS)
        def _(k):
            ar_col(e, k).wait_send()

        @pl.loop(1, ROWS)
        def _(k):
            ar_row(e, k).wait_send()

    for c in (0, 1):
        send_on(2, c).wait_send()
    for c in (2, 3):
        send_back(c).wait_send()
        send_onward(c).wait_send()

    @pl.loop(0, 4)
    def _(j):
        core_copy(j).wait_send()

        @pl.loop(1, 4)
        def _(k):
            first_z(j, k).wait_send()
            first_x(j, k).wait_send()

    for k in (1, 2, 3):
        first_y(k).wait_send()
        for step in (1, 2):
            for part in range(3):
                axis_copy(step, part, k).wait_send()
    effects_copy.wait()
    scores_copy.wait()


def body(marginal, penalty, ld_diag, ld_low, band, genotypes):
    smem = pl.BlockSpec(memory_space=pltpu.SMEM)
    hbm = pl.BlockSpec(memory_space=pl.ANY)
    big = lambda *lead: pltpu.VMEM((*lead, BS, K), F32)
    parts = []
    for _, size, order in PARTS:
        parts += [pltpu.VMEM((3, 4, 4, size, K), F32), pltpu.VMEM((3, 4, size, K), F32), pltpu.VMEM((3, size, K), F32)]
    dma = pltpu.SemaphoreType.DMA
    return pl.pallas_call(
        kernel,
        out_shape=(jax.ShapeDtypeStruct((BS, K), F32), jax.ShapeDtypeStruct((40, K), F32)),
        in_specs=[smem, hbm, hbm, hbm, hbm, hbm],
        out_specs=(hbm, hbm),
        scratch_shapes=[
            pltpu.VMEM((NC, BS, CH), F32),
            pltpu.VMEM((NC, CH, BS), F32),
            pltpu.VMEM((3, 2, BS, BS), BF16),
            pltpu.VMEM((2, 2, BS, BS), BF16),
            pltpu.VMEM((8 * GROUP, BS), BF16),
            big(3), big(3), big(3), big(),
            pltpu.VMEM((BS, 2 * K), BF16),
            pltpu.VMEM((CH, 2 * K), BF16),
            big(2), big(2), big(2), big(2), big(3), big(),
            pltpu.VMEM((1, K), F32), big(), big(), big(), big(), big(),
            pltpu.VMEM((BS, K), BF16),
            pltpu.VMEM((3, 8, K), F32),
            pltpu.VMEM((3, COLS, 8, K), F32),
            pltpu.VMEM((3, ROWS, 8, K), F32),
            pltpu.VMEM((3, 8, K), F32),
            pltpu.VMEM((4, 4, 4, 40, K), F32),
            pltpu.VMEM((4, 4, 4, 40, K), F32),
            pltpu.VMEM((4, 4, 4, 40, K), F32),
            *parts,
            *[pltpu.VMEM((4, 4, size, K), F32) for _, size, _ in PARTS],
            *[pltpu.VMEM((4, size, K), F32) for _, size, _ in PARTS],
            pltpu.VMEM((40, K), F32),
            dma((2,)), dma((NC,)), dma((NC,)), dma, dma((2,)),
            dma((3, 4, NC)), dma((3, 4, NC)),
            dma((3, 2, COLS)), dma((3, 2, COLS)),
            dma((4,)), dma((4,)),
            dma((3, 3, 4)), dma((3, 3, 4)),
            dma((2, 4, 4)), dma((2, 4, 4)),
        ],
        compiler_params=pltpu.CompilerParams(
            collective_id=0, has_side_effects=True, vmem_limit_bytes=63 * 1024 * 1024
        ),
    )(band, marginal, penalty.reshape(1, K), ld_diag, ld_low, genotypes)


def solution(mesh):
    placed = (
        P(("row", "col"), None),
        P(),
        P(("row", "col"), None, None),
        P(("row", "col"), None, None, None),
        P(("row", "col")),
        P(None, ("row", "col")),
    )
    return jax.shard_map(
        body,
        mesh=mesh,
        in_specs=placed,
        out_specs=(P(("row", "col"), None), P(("row", "col"), None)),
        check_vma=False,
    )
```

time: 126 us -> 118 us (0.937)
  Pallas kernels: 120 us -> 114 us
    pallas_call x1, Pallas kernels: 120 us -> 114 us  [body(): pl.pallas_call(kernel, out_shape=(jax.ShapeDtypeStruct((BS, K), F32), jax...]
where the time goes in v2:
time: 118 us
  Pallas kernels  114 us (97%)
  local copies, waits for them, and re-layouts  3.2 us (3%)
  between operations  1.29 us (1%)
    pallas_call x1, Pallas kernels, body(): pl.pallas_call(kernel, out_shape=(jax.ShapeDtypeStruct((BS, K), F32), jax...  114 us
    unnamed x2, local copies, waits for them, and re-layouts  3.2 us

profile of v2, /device:TPU:0, one launch (start us, length us, event | category | flops | bytes accessed | tf_op | source)
XLA Modules:
  0.0 118.1 jit_solution(10246005711081996949)
XLA Ops:
  1.3 113.6 %shard_map.77 = (f32[1024,128]{1,0:T(8,128)}, f32[40,128]{1,0:T(8,128)}) custom-call(s32[1]{0:T(128)S(6)} %copy.10.band, f32[1024,128]{1,0:T(8,128)} %marginal.1, f32[1,128]{1,0:T(1,128)} %bitcast.1, f32[1,1024,1024]{2,1,0:T(8,128)} %ld_diag.1, f32[1,2,1024,1024]{3,2,1,0:T(8,128)} %ld_low.1, bf16[5120,1024]{1,0:T(8,128)(2,1)} %genotypes.1), custom_call_target="tpu_custom_call" | custom-call | tf_op jit(solution)/shard_map/pallas_call | solution.py:523
  114.9 1.9 %copy.11 = f32[1024,128]{1,0:T(8,128)} copy(f32[1024,128]{1,0:T(8,128)} %get-tuple-element.4) | data formatting | bytes 1048576
  116.7 1.3 %copy.12 = f32[40,128]{1,0:T(8,128)} copy(f32[40,128]{1,0:T(8,128)} %get-tuple-element.5) | data formatting | bytes 40960

commit v3 on v2

v3 whole, which is shorter than its diff:
```python
import jax
import jax.numpy as jnp
from jax import lax
from jax.experimental import pallas as pl
from jax.experimental.pallas import tpu as pltpu
from jax.sharding import PartitionSpec as P

MESH = pl.DeviceIdType.MESH
F32 = jnp.float32
BF16 = jnp.bfloat16
BS = 1024
K = 128
ROWS = 8
COLS = 16
CH = 256
NC = BS // CH
GROUP = 640
PARTS = ((0, 16, "yzx"), (16, 16, "zxy"), (32, 8, "xyz"))


def split(v):
    high = v.astype(BF16)
    return high, (v - high.astype(F32)).astype(BF16)


def both(v):
    return jnp.concatenate(split(v), axis=1)


def dot(a, b):
    return jnp.dot(a, b, preferred_element_type=F32)


def product(high, low, pair):
    wide = dot(high, pair)
    return wide[:, :K] + wide[:, K:] + dot(low, pair[:, :K])


def chunk(c):
    return pl.ds(pl.multiple_of(c * CH, CH), CH)


def kernel(
    band_in, marginal, penalty_in, ld_diag, ld_low, genotypes,
    effects, scores,
    band, stage, diag_stage, tiles, flipped, geno, vec, m1, m2, via, pair, tail, u2, ru2, us, rus, look, dw,
    penalty, q1, r1, d1, d2, x01, rounded, coef, payload, ar_one, ar_two, ar_three, mid_x, mid_y,
    sc, rc, total, p0a, p0b, p0c, p1a, p1b, p1c, p2a, p2b, p2c, v0, v1, v2, w0, w1, w2, mine40,
    small_sem, load_sem, diag_sem, geno_sem, out_sem, chain_s, chain_r, ar_s, ar_r, core_s, core_r,
    rs_s, rs_r, first_s, first_r,
):
    row, col = lax.axis_index("row"), lax.axis_index("col")
    place = row * COLS + col
    y, core, x, z = row // 2, row % 2, col // 4, col % 4

    def hop(distance):
        to = (place + distance + ROWS * COLS) % (ROWS * COLS)
        return (to // COLS, to % COLS)

    def at(**new):
        p = dict(y=y, core=core, x=x, z=z)
        p.update(new)
        return (p["y"] * 2 + p["core"], p["x"] * 4 + p["z"])

    back = at(z=(z + 3) % 4)
    onward = hop(jnp.where(z == 3, -1, 3))
    from_onward = hop(jnp.where(z == 2, 1, -3))

    b_copy = pltpu.make_async_copy(marginal, vec.at[0], small_sem.at[0])
    band_copy = pltpu.make_async_copy(band_in, band, small_sem.at[2])
    penalty_copy = pltpu.make_async_copy(penalty_in, penalty, small_sem.at[1])
    geno_copy = pltpu.make_async_copy(genotypes, geno, geno_sem)

    def load(t, c):
        return pltpu.make_async_copy(ld_low.at[0, 1 - t, :, chunk(c)], stage.at[c], load_sem.at[c])

    def load_diag(c):
        return pltpu.make_async_copy(ld_diag.at[0, chunk(c)], diag_stage.at[c], diag_sem.at[c])

    band_copy.start()
    b_copy.start()
    penalty_copy.start()
    for c in range(NC):
        load(0, c).start()

    barrier = pltpu.get_barrier_semaphore()
    for device in (hop(1), hop(2), hop(-1), hop(-2), onward, from_onward):
        pl.semaphore_signal(barrier, inc=1, device_id=device, device_id_type=MESH)

    straight = [at(z=(z + k % 4) % 4, core=(core + k // 4) % 2) for k in range(1, 8)]
    straight += [at(x=(x + k) % 4) for k in (1, 2, 3)] + [at(y=(y + k) % 4) for k in (1, 2, 3)]
    for device in straight:
        pl.semaphore_signal(barrier, inc=1, device_id=device, device_id_type=MESH)

    b_copy.wait()
    band_copy.wait()
    pl.semaphore_wait(barrier, 6 + len(straight))

    def remote(src, dst, send, recv, device):
        return pltpu.make_async_remote_copy(
            src_ref=src, dst_ref=dst, send_sem=send, recv_sem=recv,
            device_id=device, device_id_type=MESH,
        )

    def send_own(e, c):
        return remote(vec.at[e, chunk(c)], m1.at[e, chunk(c)],
                      chain_s.at[e, 0, c], chain_r.at[e, 0, c], hop(1))

    def send_on(e, c):
        return remote(m1.at[e, chunk(c)], m2.at[e, chunk(c)],
                      chain_s.at[e, 1, c], chain_r.at[e, 1, c], hop(1))

    def send_u2(e, c):
        return remote(u2.at[e, chunk(c)], ru2.at[e, chunk(c)],
                      chain_s.at[e, 2, c], chain_r.at[e, 2, c], hop(-1))

    def send_us(e, c):
        return remote(us.at[e, chunk(c)], rus.at[e, chunk(c)],
                      chain_s.at[e, 3, c], chain_r.at[e, 3, c], hop(-1))

    def send_back(c):
        return remote(vec.at[2, chunk(c)], via.at[chunk(c)],
                      chain_s.at[2, 2, c], chain_r.at[2, 2, c], back)

    def send_onward(c):
        return remote(via.at[chunk(c)], m2.at[2, chunk(c)],
                      chain_s.at[2, 3, c], chain_r.at[2, 3, c], onward)

    @pl.loop(0, NC)
    def _(c):
        send_own(0, c).start()

    for c in range(NC):
        load_diag(c).start()

    place_f = [place >= distance for distance in (1, 2)]
    active = [
        jnp.where(jnp.logical_and(place_f[d - 1], band[0] >= d), 1.0, 0.0).astype(F32) for d in (1, 2)
    ]

    def convert(t, c):
        load(t, c).wait()
        block = stage[c] * active[1 - t]
        high, low = split(block)
        tiles[t, 0, :, chunk(c)] = high
        tiles[t, 1, :, chunk(c)] = low
        high, low = split(block.T)
        flipped[t, 0, chunk(c), :] = high
        flipped[t, 1, chunk(c), :] = low
        if t == 0:
            load(1, c).start()

    def ar_copy(n, stage_no, k):
        src = (payload, mid_x, mid_y)[stage_no].at[n]
        if stage_no == 0:
            device = at(z=(z + k % 4) % 4, core=(core + k // 4) % 2)
        elif stage_no == 1:
            device = at(x=(x + k) % 4)
        else:
            device = at(y=(y + k) % 4)
        return remote(src, (ar_one, ar_two, ar_three)[stage_no].at[n, k],
                      ar_s.at[n, stage_no, k], ar_r.at[n, stage_no, k], device)

    def ar_send(n, stage_no):
        for k in range(1, (8, 4, 4)[stage_no]):
            ar_copy(n, stage_no, k).start()

    def ar_sum(n, stage_no):
        acc = (payload, mid_x, mid_y)[stage_no][n]
        for k in range(1, (8, 4, 4)[stage_no]):
            ar_copy(n, stage_no, k).wait_recv()
            acc = acc + (ar_one, ar_two, ar_three)[stage_no][n, k]
        return acc

    def ar_next(n, stage_no):
        (mid_x, mid_y)[stage_no][n] = ar_sum(n, stage_no)
        ar_send(n, stage_no + 1)

    def column(v):
        return jnp.sum(v, axis=0, keepdims=True)

    def over_chunks(n, body, count):
        zero = jnp.zeros((1, K), F32)
        sums = lax.fori_loop(0, NC, body, (zero,) * count)
        for j in range(count):
            payload[n, j : j + 1, :] = sums[j]

    def add_second(e, c):
        tail[...] = both(m2[e, chunk(c), :])

        @pl.loop(0, NC)
        def _(r):
            look[e, chunk(r), :] = below(e, r, c)

    def below(e, r, c):
        return look[e, chunk(r), :] + product(
            tiles[0, 0, chunk(r), chunk(c)], tiles[0, 1, chunk(r), chunk(c)], tail[...]
        )

    def add_first(e, c):
        tail[...] = both(m1[e, chunk(c), :])

        @pl.loop(0, NC)
        def _(r):
            part = product(tiles[1, 0, chunk(r), chunk(c)], tiles[1, 1, chunk(r), chunk(c)], tail[...])
            look[e, chunk(r), :] = jnp.where(c == 0, part, part + look[e, chunk(r), :])

    def diagonal(e):
        @pl.loop(0, NC)
        def _(c):
            @pl.when(e == 0)
            def _():
                load_diag(c).wait()
                high, low = split(diag_stage[c])
                tiles[2, 0, chunk(c), :] = high
                tiles[2, 1, chunk(c), :] = low

            dw[chunk(c), :] = (
                product(tiles[2, 0, chunk(c), :], tiles[2, 1, chunk(c), :], pair[...])
                + penalty[...] * vec[e, chunk(c), :]
            )

    def sums_one():
        def go(c, sums):
            here, out = vec[0, chunk(c), :], vec[1, chunk(c), :]
            return (sums[0] + column(here * here), sums[1] + column(here * out), sums[2] + column(out * out))

        over_chunks(0, go, 3)

    def solve_one():
        got = ar_sum(0, 2)
        bb, bq, qq = got[0:1], got[1:2], got[2:3]
        alpha = bb / bq
        after = jnp.maximum(bb - 2.0 * alpha * bq + alpha * alpha * qq, 0.0)
        coef[0:1, :] = alpha
        coef[1:2, :] = after / bb

    def sums_two():
        a0, b1 = coef[0:1, :], coef[1:2, :]

        def go(c, sums):
            here, q, s = vec[0, chunk(c), :], vec[1, chunk(c), :], vec[2, chunk(c), :]
            res = here - a0 * q
            direction = res + b1 * here
            image = (1.0 + b1) * q - a0 * s
            r1[chunk(c), :] = res
            d1[chunk(c), :] = direction
            q1[chunk(c), :] = image
            terms = (res * res, res * direction, direction * image, res * image, image * image)
            return tuple(t + column(v) for t, v in zip(sums, terms))

        over_chunks(1, go, 5)

    def solve_two():
        got = ar_sum(1, 2)
        rr, rd, dq, rq, qq = (got[j : j + 1] for j in range(5))
        a0 = coef[0:1, :]
        a1 = rd / dq
        after = jnp.maximum(rr - 2.0 * a1 * rq + a1 * a1 * qq, 0.0)
        b2 = after / rr
        coef[2:3, :] = a1
        coef[3:4, :] = b2

        @pl.loop(0, NC)
        def _(c):
            res = r1[chunk(c), :] - a1 * q1[chunk(c), :]
            r1[chunk(c), :] = res
            d2[chunk(c), :] = res + b2 * d1[chunk(c), :]
            x01[chunk(c), :] = a0 * vec[0, chunk(c), :] + a1 * d1[chunk(c), :]

    def sums_three():
        a0, b1, a1, b2 = (coef[j : j + 1, :] for j in range(4))
        c0 = 1.0 + b2 * (1.0 + b1)
        c1 = -a0 - a1 * (1.0 + b1) - b2 * a0
        c2 = a1 * a0

        def go(c, sums):
            direction = d2[chunk(c), :]
            image = c0 * look[0, chunk(c), :] + c1 * look[1, chunk(c), :] + c2 * look[2, chunk(c), :]
            return (sums[0] + column(r1[chunk(c), :] * direction), sums[1] + column(direction * image))

        over_chunks(2, go, 2)

    @pl.loop(0, NC)
    def _(c):
        pair[chunk(c), :] = both(vec[0, chunk(c), :])

    payload[...] = jnp.zeros_like(payload)
    penalty_copy.wait()

    @pl.loop(0, 3)
    def _(e):
        @pl.when(e == 2)
        def _():
            send_back(2).start()
            send_back(3).start()

        @pl.when(e < 2)
        def _():
            @pl.loop(0, NC)
            def _(c):
                @pl.when(e == 0)
                def _():
                    convert(0, c)

                u2[e, chunk(c), :] = product(flipped[0, 0, chunk(c), :], flipped[0, 1, chunk(c), :], pair[...])
                send_u2(e, c).start()

        @pl.when(e == 1)
        def _():
            sums_one()
            ar_send(0, 0)

        @pl.when(e == 2)
        def _():
            sums_two()
            ar_send(1, 0)

        @pl.loop(0, NC)
        def _(c):
            send_own(e, c).wait_recv()

            @pl.when(jnp.logical_or(e < 2, c < 2))
            def _():
                send_on(e, c).start()

            @pl.when(jnp.logical_and(e == 2, c >= 2))
            def _():
                send_back(c).wait_recv()
                send_onward(c).start()

            @pl.when(e == 0)
            def _():
                convert(1, c)

            @pl.when(e < 2)
            def _():
                up = product(flipped[1, 0, chunk(c), :], flipped[1, 1, chunk(c), :], pair[...])
                send_u2(e, c).wait_recv()
                us[e, chunk(c), :] = up + ru2[e, chunk(c), :]
                send_us(e, c).start()

            add_first(e, c)

        @pl.when(e == 0)
        def _():
            geno_copy.start()

        @pl.when(e > 0)
        def _():
            ar_next(e - 1, 0)

        diagonal(e)

        @pl.when(e > 0)
        def _():
            ar_next(e - 1, 1)

        def turn(i):
            return jnp.where(e == 2, (i + 2) % NC, i)

        def wait_second(c):
            @pl.when(jnp.logical_or(e < 2, c < 2))
            def _():
                send_on(e, c).wait_recv()

            @pl.when(jnp.logical_and(e == 2, c >= 2))
            def _():
                send_onward(c).wait_recv()

        @pl.loop(0, NC - 1)
        def _(i):
            wait_second(turn(i))
            add_second(e, turn(i))

        @pl.when(e == 1)
        def _():
            solve_one()

        @pl.when(e == 2)
        def _():
            solve_two()

        last = turn(NC - 1)
        wait_second(last)
        tail[...] = both(m2[e, chunk(last), :])

        @pl.loop(0, NC)
        def _(r):
            down = below(e, r, last)
            part = dw[chunk(r), :]
            look[e, chunk(r), :] = part + 2.0 * down

            @pl.when(e < 2)
            def _():
                send_us(e, r).wait_recv()
                out = part + down + rus[e, chunk(r), :]
                vec[e + 1, chunk(r), :] = out
                send_own(e + 1, r).start()
                pair[chunk(r), :] = both(out)

    sums_three()
    ar_send(2, 0)
    geno_copy.wait()
    ar_next(2, 0)
    ar_next(2, 1)
    got = ar_sum(2, 2)
    a2 = got[0:1] / got[1:2]

    @pl.loop(0, NC)
    def _(c):
        value = x01[chunk(c), :] + a2 * d2[chunk(c), :]
        x01[chunk(c), :] = value
        rounded[chunk(c), :] = value.astype(BF16)

    effects_copy = pltpu.make_async_copy(x01, effects, out_sem.at[0])
    effects_copy.start()

    def people(j, which):
        rows = pl.ds(pl.multiple_of((j * 2 + which) * GROUP, GROUP), GROUP)
        return dot(geno[rows, :], rounded[...]).reshape(4, 4, 40, K)

    def core_copy(j):
        return remote(sc.at[j], rc.at[j], core_s.at[j], core_r.at[j], at(core=1 - core))

    def rows_of(part):
        return pl.ds(PARTS[part][0], PARTS[part][1])

    def first_y(k):
        to = (y + k) % 4
        return remote(total.at[to, :, :, rows_of(0), :], p0a.at[k - 1], rs_s.at[0, 0, k], rs_r.at[0, 0, k], at(y=to))

    def first_z(j, k):
        to = (z + k) % 4
        return remote(total.at[j, :, to, rows_of(1), :], p1a.at[k - 1, j], first_s.at[0, k, j], first_r.at[0, k, j], at(z=to))

    def first_x(j, k):
        to = (x + k) % 4
        return remote(total.at[j, to, :, rows_of(2), :], p2a.at[k - 1, j], first_s.at[1, k, j], first_r.at[1, k, j], at(x=to))

    def other_core(n):
        j = (y + n) % 4
        sc[j] = people(j, 1 - core)
        core_copy(j).start()

    def own_core(n):
        j = (y + n) % 4
        mine = people(j, core)
        core_copy(j).wait_recv()
        total[j] = mine + rc[j]
        @pl.when(n > 0)
        def _():
            first_y(n).start()

        for k in (1, 3, 2):
            first_z(j, k).start()
            first_x(j, k).start()

    @pl.loop(0, 5)
    def _(i):
        @pl.when(i < 4)
        def _():
            other_core((i + 1) % 4)

        @pl.when(i > 0)
        def _():
            own_core(i % 4)

    landed = ((p0a, p0b, p0c), (p1a, p1b, p1c), (p2a, p2b, p2c))
    halfway = ((v0, w0), (v1, w1), (v2, w2))

    def axis_copy(step, part, k):
        order = PARTS[part][2]
        axis = order[step]
        to = (dict(y=y, x=x, z=z)[axis] + k) % 4
        ref = halfway[part][step - 1]
        left = [a for a in "yxz" if a != order[0]]
        src = ref.at[:, to] if step == 1 and left[1] == axis else ref.at[to]
        return remote(src, landed[part][step].at[k - 1], rs_s.at[step, part, k], rs_r.at[step, part, k], at(**{axis: to}))

    def send_axis(step, part):
        for k in (1, 3, 2):
            axis_copy(step, part, k).start()

    for part in (2, 0, 1):
        for k in (1, 3, 2):
            if part == 0:
                first_y(k).wait_recv()
            else:
                for n in (1, 2, 3, 0):
                    (first_z, first_x)[part - 1]((y + n) % 4, k).wait_recv()

        @pl.loop(0, 4)
        def _(i):
            acc = (
                lambda: total[y, i, :, rows_of(0), :],
                lambda: total[i, :, z, rows_of(1), :],
                lambda: total[i, x, :, rows_of(2), :],
            )[part]()
            for k in (1, 3, 2):
                acc = acc + landed[part][0][k - 1, i]
            halfway[part][0][i] = acc

        send_axis(1, part)
    for step in (1, 2):
        for part in (2, 0, 1):
            order = PARTS[part][2]
            axis = order[step]
            mine = dict(y=y, x=x, z=z)[axis]
            ref = halfway[part][step - 1]
            left = [a for a in "yxz" if a != order[0]]
            acc = ref[:, mine] if step == 1 and left[1] == axis else ref[mine]
            for k in (1, 3, 2):
                axis_copy(step, part, k).wait_recv()
                acc = acc + landed[part][step][k - 1]
            if step == 1:
                halfway[part][1][...] = acc
                send_axis(2, part)
            else:
                mine40[rows_of(part), :] = acc

    scores_copy = pltpu.make_async_copy(mine40, scores, out_sem.at[1])
    scores_copy.start()

    for e in range(3):
        @pl.loop(0, NC)
        def _(c):
            send_own(e, c).wait_send()
            if e < 2:
                send_on(e, c).wait_send()
                send_u2(e, c).wait_send()
                send_us(e, c).wait_send()

        for stage_no in range(3):
            for k in range(1, (8, 4, 4)[stage_no]):
                ar_copy(e, stage_no, k).wait_send()

    for c in (0, 1):
        send_on(2, c).wait_send()
    for c in (2, 3):
        send_back(c).wait_send()
        send_onward(c).wait_send()

    @pl.loop(0, 4)
    def _(j):
        core_copy(j).wait_send()

        @pl.loop(1, 4)
        def _(k):
            first_z(j, k).wait_send()
            first_x(j, k).wait_send()

    for k in (1, 2, 3):
        first_y(k).wait_send()
        for step in (1, 2):
            for part in range(3):
                axis_copy(step, part, k).wait_send()
    effects_copy.wait()
    scores_copy.wait()


def body(marginal, penalty, ld_diag, ld_low, band, genotypes):
    hbm = pl.BlockSpec(memory_space=pl.ANY)
    big = lambda *lead: pltpu.VMEM((*lead, BS, K), F32)
    parts = []
    for _, size, order in PARTS:
        parts += [pltpu.VMEM((3, 4, 4, size, K), F32), pltpu.VMEM((3, 4, size, K), F32), pltpu.VMEM((3, size, K), F32)]
    dma = pltpu.SemaphoreType.DMA
    return pl.pallas_call(
        kernel,
        out_shape=(jax.ShapeDtypeStruct((BS, K), F32), jax.ShapeDtypeStruct((40, K), F32)),
        in_specs=[hbm, hbm, hbm, hbm, hbm, hbm],
        out_specs=(hbm, hbm),
        scratch_shapes=[
            pltpu.SMEM((1,), jnp.int32),
            pltpu.VMEM((NC, BS, CH), F32),
            pltpu.VMEM((NC, CH, BS), F32),
            pltpu.VMEM((3, 2, BS, BS), BF16),
            pltpu.VMEM((2, 2, BS, BS), BF16),
            pltpu.VMEM((8 * GROUP, BS), BF16),
            big(3), big(3), big(3), big(),
            pltpu.VMEM((BS, 2 * K), BF16),
            pltpu.VMEM((CH, 2 * K), BF16),
            big(2), big(2), big(2), big(2), big(3), big(),
            pltpu.VMEM((1, K), F32), big(), big(), big(), big(), big(),
            pltpu.VMEM((BS, K), BF16),
            pltpu.VMEM((8, K), F32),
            pltpu.VMEM((3, 8, K), F32),
            pltpu.VMEM((3, 8, 8, K), F32),
            pltpu.VMEM((3, 4, 8, K), F32),
            pltpu.VMEM((3, 4, 8, K), F32),
            pltpu.VMEM((3, 8, K), F32),
            pltpu.VMEM((3, 8, K), F32),
            pltpu.VMEM((4, 4, 4, 40, K), F32),
            pltpu.VMEM((4, 4, 4, 40, K), F32),
            pltpu.VMEM((4, 4, 4, 40, K), F32),
            *parts,
            *[pltpu.VMEM((4, 4, size, K), F32) for _, size, _ in PARTS],
            *[pltpu.VMEM((4, size, K), F32) for _, size, _ in PARTS],
            pltpu.VMEM((40, K), F32),
            dma((3,)), dma((NC,)), dma((NC,)), dma, dma((2,)),
            dma((3, 4, NC)), dma((3, 4, NC)),
            dma((3, 3, 8)), dma((3, 3, 8)),
            dma((4,)), dma((4,)),
            dma((3, 3, 4)), dma((3, 3, 4)),
            dma((2, 4, 4)), dma((2, 4, 4)),
        ],
        compiler_params=pltpu.CompilerParams(
            collective_id=0, has_side_effects=True, vmem_limit_bytes=63 * 1024 * 1024
        ),
    )(band, marginal, penalty.reshape(1, K), ld_diag, ld_low, genotypes)


def solution(mesh):
    placed = (
        P(("row", "col"), None),
        P(),
        P(("row", "col"), None, None),
        P(("row", "col"), None, None, None),
        P(("row", "col")),
        P(None, ("row", "col")),
    )
    return jax.shard_map(
        body,
        mesh=mesh,
        in_specs=placed,
        out_specs=(P(("row", "col"), None), P(("row", "col"), None)),
        check_vma=False,
    )
```

time: 118 us -> 131 us (1.11)
  Pallas kernels: 114 us -> 126 us
    pallas_call x1, Pallas kernels: 114 us -> 126 us  [body(): pl.pallas_call(kernel, out_shape=(jax.ShapeDtypeStruct((BS, K), F32), jax...]
where the time goes in v3:
time: 131 us
  Pallas kernels  126 us (96%)
  local copies, waits for them, and re-layouts  3.2 us (2%)
    pallas_call x1, Pallas kernels, body(): pl.pallas_call(kernel, out_shape=(jax.ShapeDtypeStruct((BS, K), F32), jax...  126 us
    unnamed x2, local copies, waits for them, and re-layouts  3.2 us

profile of v3, /device:TPU:0, one launch (start us, length us, event | category | flops | bytes accessed | tf_op | source)
XLA Modules:
  0.0 130.7 jit_solution(2435296220634372693)
XLA Ops:
  1.3 126.2 %shard_map.77 = (f32[1024,128]{1,0:T(8,128)}, f32[40,128]{1,0:T(8,128)}) custom-call(s32[1]{0:T(128)S(6)} %copy.10.band_in, f32[1024,128]{1,0:T(8,128)} %marginal.1, f32[1,128]{1,0:T(1,128)} %bitcast.1, f32[1,1024,1024]{2,1,0:T(8,128)} %ld_diag.1, f32[1,2,1024,1024]{3,2,1,0:T(8,128)} %ld_low.1, bf16[5120,1024]{1,0:T(8,128)(2,1)} %genotypes.1), custom_call_target="tpu_custom_call" | custom-call | tf_op jit(solution)/shard_map/pallas_call | solution.py:569
  127.5 1.9 %copy.11 = f32[1024,128]{1,0:T(8,128)} copy(f32[1024,128]{1,0:T(8,128)} %get-tuple-element.4) | data formatting | bytes 1048576
  129.3 1.3 %copy.12 = f32[40,128]{1,0:T(8,128)} copy(f32[40,128]{1,0:T(8,128)} %get-tuple-element.5) | data formatting | bytes 40960

commit v4 on v2

--- a/solution.py
+++ b/solution.py
@@ -41,13 +41,13 @@
 
 
 def kernel(
-    band, marginal, penalty_in, ld_diag, ld_low, genotypes,
+    band_in, marginal, penalty_in, ld_diag, ld_low, genotypes,
     effects, scores,
-    stage, diag_stage, tiles, flipped, geno, vec, m1, m2, via, pair, tail, u2, ru2, us, rus, look, dw,
+    band, stage, diag_stage, tiles, flipped, geno, vec, m1, m2, via, pair, tail, u2, ru2, us, rus, look, dw,
     penalty, q1, r1, d1, d2, x01, rounded, payload, ar_one, ar_two, mid,
     sc, rc, total, p0a, p0b, p0c, p1a, p1b, p1c, p2a, p2b, p2c, v0, v1, v2, w0, w1, w2, mine40,
-    small_sem, load_sem, diag_sem, geno_sem, out_sem, chain_s, chain_r, ar_s, ar_r, core_s, core_r,
-    rs_s, rs_r, first_s, first_r,
+    small_sem, load_sem, diag_sem, geno_sem, out_sem, chain_s, chain_r, up_r, via_r, ar_s, ar_r, core_s, core_r,
+    rs_s, rs_r,
 ):
     row, col = lax.axis_index("row"), lax.axis_index("col")
     place = row * COLS + col
@@ -67,6 +67,7 @@
     from_onward = hop(jnp.where(z == 2, 1, -3))
 
     b_copy = pltpu.make_async_copy(marginal, vec.at[0], small_sem.at[0])
+    band_copy = pltpu.make_async_copy(band_in, band, small_sem.at[2])
     penalty_copy = pltpu.make_async_copy(penalty_in, penalty, small_sem.at[1])
     geno_copy = pltpu.make_async_copy(genotypes, geno, geno_sem)
 
@@ -76,6 +77,7 @@
     def load_diag(c):
         return pltpu.make_async_copy(ld_diag.at[0, chunk(c)], diag_stage.at[c], diag_sem.at[c])
 
+    band_copy.start()
     b_copy.start()
     penalty_copy.start()
     for c in range(NC):
@@ -94,6 +96,7 @@
         pl.semaphore_signal(barrier, inc=1, device_id=((row + k) % ROWS, col), device_id_type=MESH)
 
     b_copy.wait()
+    band_copy.wait()
     pl.semaphore_wait(barrier, 6 + COLS - 1 + ROWS - 1)
 
     def remote(src, dst, send, recv, device):
@@ -104,27 +107,27 @@
 
     def send_own(e, c):
         return remote(vec.at[e, chunk(c)], m1.at[e, chunk(c)],
-                      chain_s.at[e, 0, c], chain_r.at[e, 0, c], hop(1))
+                      chain_s.at[0], chain_r.at[e, 0, c], hop(1))
 
     def send_on(e, c):
         return remote(m1.at[e, chunk(c)], m2.at[e, chunk(c)],
-                      chain_s.at[e, 1, c], chain_r.at[e, 1, c], hop(1))
+                      chain_s.at[1 if e < 2 else 2], chain_r.at[e, 1, c], hop(1))
 
     def send_u2(e, c):
         return remote(u2.at[e, chunk(c)], ru2.at[e, chunk(c)],
-                      chain_s.at[e, 2, c], chain_r.at[e, 2, c], hop(-1))
+                      chain_s.at[3], up_r.at[e, 0, c], hop(-1))
 
     def send_us(e, c):
         return remote(us.at[e, chunk(c)], rus.at[e, chunk(c)],
-                      chain_s.at[e, 3, c], chain_r.at[e, 3, c], hop(-1))
+                      chain_s.at[4], up_r.at[e, 1, c], hop(-1))
 
     def send_back(c):
         return remote(vec.at[2, chunk(c)], via.at[chunk(c)],
-                      chain_s.at[2, 2, c], chain_r.at[2, 2, c], back)
+                      chain_s.at[5], via_r.at[c - 2], back)
 
     def send_onward(c):
         return remote(via.at[chunk(c)], m2.at[2, chunk(c)],
-                      chain_s.at[2, 3, c], chain_r.at[2, 3, c], onward)
+                      chain_s.at[6], chain_r.at[2, 1, c], onward)
 
     @pl.loop(0, NC)
     def _(c):
@@ -150,45 +153,35 @@
         if t == 0:
             load(1, c).start()
 
-    def ar_col(n, k):
-        return remote(payload.at[n], ar_one.at[n, k], ar_s.at[n, 0, k], ar_r.at[n, 0, k],
-                      (row, (col + k) % COLS))
-
-    def ar_row(n, k):
-        return remote(mid.at[n], ar_two.at[n, k], ar_s.at[n, 1, k], ar_r.at[n, 1, k],
-                      ((row + k) % ROWS, col))
+    def ar_copy(n, step, k):
+        if step == 0:
+            return remote(payload.at[n], ar_one.at[n, k - 1], ar_s.at[0], ar_r.at[n, 0], (row, (col + k) % COLS))
+        return remote(mid.at[n], ar_two.at[n, k - 1], ar_s.at[1], ar_r.at[n, 1], ((row + k) % ROWS, col))
+
+    def ar_all(n, step):
+        ref = (ar_one, ar_two)[step].at[n]
+        return remote(ref, ref, ar_s.at[step], ar_r.at[n, step], hop(1))
+
+    def ar_send(n, step):
+        @pl.loop(1, (COLS, ROWS)[step])
+        def _(k):
+            ar_copy(n, step, k).start()
 
     def ar_start(n, rows):
         for j in range(8):
             payload[n, j : j + 1, :] = rows[j] if j < len(rows) else jnp.zeros((1, K), F32)
-
-        @pl.loop(1, COLS)
-        def _(k):
-            ar_col(n, k).start()
-
-    def ar_middle(n):
-        @pl.loop(1, COLS)
-        def _(k):
-            ar_col(n, k).wait_recv()
-
-        acc = payload[n]
-        for k in range(1, COLS):
-            acc = acc + ar_one[n, k]
-        mid[n] = acc
-
-        @pl.loop(1, ROWS)
-        def _(k):
-            ar_row(n, k).start()
-
-    def ar_end(n):
-        @pl.loop(1, ROWS)
-        def _(k):
-            ar_row(n, k).wait_recv()
-
-        acc = mid[n]
-        for k in range(1, ROWS):
-            acc = acc + ar_two[n, k]
+        ar_send(n, 0)
+
+    def ar_sum(n, step):
+        ar_all(n, step).wait_recv()
+        acc = (payload, mid)[step][n]
+        for k in range(1, (COLS, ROWS)[step]):
+            acc = acc + (ar_one, ar_two)[step][n, k - 1]
         return acc
+
+    def ar_next(n):
+        mid[n] = ar_sum(n, 0)
+        ar_send(n, 1)
 
     def column(v):
         return jnp.sum(v, axis=0, keepdims=True)
@@ -228,7 +221,7 @@
                 + penalty[...] * vec[e, chunk(c), :]
             )
 
-    def exchange(e, early, middle, late):
+    def exchange(e, early, middle, between, late):
         @pl.loop(0, NC)
         def _(c):
             if e == 0:
@@ -252,13 +245,14 @@
 
         middle()
         diagonal(e)
-        late()
+        between()
 
         @pl.loop(0, NC - 1)
         def _(c):
             send_on(e, c).wait_recv()
             add_second(e, c)
 
+        late()
         send_on(e, NC - 1).wait_recv()
         tail[...] = both(m2[e, chunk(NC - 1), :])
 
@@ -278,7 +272,7 @@
         pair[chunk(c), :] = both(vec[0, chunk(c), :])
 
     penalty_copy.wait()
-    exchange(0, lambda: None, geno_copy.start, lambda: None)
+    exchange(0, lambda: None, geno_copy.start, lambda: None, lambda: None)
 
     def one(c, sums):
         out = finish(0, c)
@@ -290,18 +284,25 @@
     coef = {}
 
     def late_one():
-        got = ar_end(0)
+        got = ar_sum(0, 1)
         bb, bq, qq = got[0:1], got[1:2], got[2:3]
         alpha = bb / bq
         after = jnp.maximum(bb - 2.0 * alpha * bq + alpha * alpha * qq, 0.0)
         coef["a0"], coef["b1"] = alpha, after / bb
 
-    exchange(1, lambda: ar_start(0, sums_one), lambda: ar_middle(0), late_one)
+    exchange(1, lambda: ar_start(0, sums_one), lambda: ar_next(0), lambda: None, lambda: None)
+
+    @pl.loop(0, NC)
+    def _(c):
+        finish(1, c)
+
+    for c in (2, 3):
+        send_back(c).start()
+    late_one()
     a0, b1 = coef["a0"], coef["b1"]
 
     def two(c, sums):
-        s = finish(1, c)
-        here, q = vec[0, chunk(c), :], vec[1, chunk(c), :]
+        here, q, s = vec[0, chunk(c), :], vec[1, chunk(c), :], vec[2, chunk(c), :]
         res = here - a0 * q
         direction = res + b1 * here
         image = (1.0 + b1) * q - a0 * s
@@ -312,8 +313,6 @@
         return tuple(t + column(v) for t, v in zip(sums, terms))
 
     sums_two = over_chunks(two, 5)
-    for c in (2, 3):
-        send_back(c).start()
     ar_start(1, sums_two)
 
     for c in range(NC):
@@ -324,9 +323,12 @@
             send_back(c).wait_recv()
             send_onward(c).start()
         add_first(2, c)
-    ar_middle(1)
+    ar_next(1)
     diagonal(2)
-    got = ar_end(1)
+    for c in (2, 3):
+        send_onward(c).wait_recv()
+        add_second(2, c)
+    got = ar_sum(1, 1)
     rr, rd, dq, rq, qq = (got[j : j + 1] for j in range(5))
     a1 = rd / dq
     after = jnp.maximum(rr - 2.0 * a1 * rq + a1 * a1 * qq, 0.0)
@@ -344,9 +346,6 @@
     c1 = -a0 - a1 * (1.0 + b1) - b2 * a0
     c2 = a1 * a0
 
-    for c in (2, 3):
-        send_onward(c).wait_recv()
-        add_second(2, c)
     send_on(2, 0).wait_recv()
     add_second(2, 0)
     send_on(2, 1).wait_recv()
@@ -360,8 +359,8 @@
     dq2 = over_chunks(three, 1)[0]
     ar_start(2, (rd2, dq2))
     geno_copy.wait()
-    ar_middle(2)
-    got = ar_end(2)
+    ar_next(2)
+    got = ar_sum(2, 1)
     a2 = got[0:1] / got[1:2]
 
     @pl.loop(0, NC)
@@ -378,22 +377,22 @@
         return dot(geno[rows, :], rounded[...]).reshape(4, 4, 40, K)
 
     def core_copy(j):
-        return remote(sc.at[j], rc.at[j], core_s.at[j], core_r.at[j], at(core=1 - core))
+        return remote(sc.at[j], rc.at[j], core_s, core_r.at[j], at(core=1 - core))
 
     def rows_of(part):
         return pl.ds(PARTS[part][0], PARTS[part][1])
 
     def first_y(k):
         to = (y + k) % 4
-        return remote(total.at[to, :, :, rows_of(0), :], p0a.at[k - 1], rs_s.at[0, 0, k], rs_r.at[0, 0, k], at(y=to))
+        return remote(total.at[to, :, :, rows_of(0), :], p0a.at[k - 1], rs_s.at[0, 0], rs_r.at[0, 0], at(y=to))
 
     def first_z(j, k):
         to = (z + k) % 4
-        return remote(total.at[j, :, to, rows_of(1), :], p1a.at[k - 1, j], first_s.at[0, k, j], first_r.at[0, k, j], at(z=to))
+        return remote(total.at[j, :, to, rows_of(1), :], p1a.at[k - 1, j], rs_s.at[0, 1], rs_r.at[0, 1], at(z=to))
 
     def first_x(j, k):
         to = (x + k) % 4
-        return remote(total.at[j, to, :, rows_of(2), :], p2a.at[k - 1, j], first_s.at[1, k, j], first_r.at[1, k, j], at(x=to))
+        return remote(total.at[j, to, :, rows_of(2), :], p2a.at[k - 1, j], rs_s.at[0, 2], rs_r.at[0, 2], at(x=to))
 
     def other_core(n):
         j = (y + n) % 4
@@ -430,7 +429,11 @@
         ref = halfway[part][step - 1]
         left = [a for a in "yxz" if a != order[0]]
         src = ref.at[:, to] if step == 1 and left[1] == axis else ref.at[to]
-        return remote(src, landed[part][step].at[k - 1], rs_s.at[step, part, k], rs_r.at[step, part, k], at(**{axis: to}))
+        return remote(src, landed[part][step].at[k - 1], rs_s.at[step, part], rs_r.at[step, part], at(**{axis: to}))
+
+    def landing(step, part):
+        ref = landed[part][step]
+        return remote(ref, ref, rs_s.at[step, part], rs_r.at[step, part], hop(1))
 
     def send_axis(step, part):
         for k in (1, 3, 2):
@@ -442,12 +445,8 @@
             lambda: total[:, :, z, rows_of(1), :],
             lambda: total[:, x, :, rows_of(2), :],
         )[part]()
+        landing(0, part).wait_recv()
         for k in (1, 3, 2):
-            if part == 0:
-                first_y(k).wait_recv()
-            else:
-                for n in (1, 3, 2, 0):
-                    (first_z, first_x)[part - 1]((y + n) % 4, k).wait_recv()
             acc = acc + landed[part][0][k - 1]
         halfway[part][0][...] = acc
         send_axis(1, part)
@@ -459,8 +458,8 @@
             ref = halfway[part][step - 1]
             left = [a for a in "yxz" if a != order[0]]
             acc = ref[:, mine] if step == 1 and left[1] == axis else ref[mine]
+            landing(step, part).wait_recv()
             for k in (1, 3, 2):
-                axis_copy(step, part, k).wait_recv()
                 acc = acc + landed[part][step][k - 1]
             if step == 1:
                 halfway[part][1][...] = acc
@@ -471,61 +470,46 @@
     scores_copy = pltpu.make_async_copy(mine40, scores, out_sem.at[1])
     scores_copy.start()
 
-    for e in range(3):
-        @pl.loop(0, NC)
-        def _(c):
-            send_own(e, c).wait_send()
-            if e < 2:
-                send_on(e, c).wait_send()
-                send_u2(e, c).wait_send()
-                send_us(e, c).wait_send()
-
-        @pl.loop(1, COLS)
-        def _(k):
-            ar_col(e, k).wait_send()
-
-        @pl.loop(1, ROWS)
-        def _(k):
-            ar_row(e, k).wait_send()
-
-    for c in (0, 1):
-        send_on(2, c).wait_send()
-    for c in (2, 3):
-        send_back(c).wait_send()
-        send_onward(c).wait_send()
-
-    @pl.loop(0, 4)
-    def _(j):
-        core_copy(j).wait_send()
-
-        @pl.loop(1, 4)
-        def _(k):
-            first_z(j, k).wait_send()
-            first_x(j, k).wait_send()
-
-    for k in (1, 2, 3):
-        first_y(k).wait_send()
-        for step in (1, 2):
-            for part in range(3):
-                axis_copy(step, part, k).wait_send()
+    def gone(ref, sem):
+        remote(ref, ref, sem, sem, hop(1)).wait_send()
+
+    gone(vec, chain_s.at[0])
+    gone(m1.at[pl.ds(0, 2)], chain_s.at[1])
+    gone(m1.at[2, pl.ds(0, 2 * CH)], chain_s.at[2])
+    gone(u2, chain_s.at[3])
+    gone(us, chain_s.at[4])
+    gone(via.at[pl.ds(2 * CH, 2 * CH)], chain_s.at[5])
+    gone(via.at[pl.ds(2 * CH, 2 * CH)], chain_s.at[6])
+    for step, ref in enumerate((ar_one, ar_two)):
+        gone(ref, ar_s.at[step])
+    gone(sc, core_s)
+    for step in range(3):
+        for part in range(3):
+            gone(landed[part][step], rs_s.at[step, part])
     effects_copy.wait()
     scores_copy.wait()
 
 
+def copy_out(effects_in, scores_in, effects, scores):
+    effects[...] = effects_in[...]
+    scores[...] = scores_in[...]
+
+
 def body(marginal, penalty, ld_diag, ld_low, band, genotypes):
-    smem = pl.BlockSpec(memory_space=pltpu.SMEM)
     hbm = pl.BlockSpec(memory_space=pl.ANY)
     big = lambda *lead: pltpu.VMEM((*lead, BS, K), F32)
     parts = []
     for _, size, order in PARTS:
         parts += [pltpu.VMEM((3, 4, 4, size, K), F32), pltpu.VMEM((3, 4, size, K), F32), pltpu.VMEM((3, size, K), F32)]
     dma = pltpu.SemaphoreType.DMA
-    return pl.pallas_call(
+    shapes = (jax.ShapeDtypeStruct((BS, K), F32), jax.ShapeDtypeStruct((40, K), F32))
+    results = pl.pallas_call(
         kernel,
-        out_shape=(jax.ShapeDtypeStruct((BS, K), F32), jax.ShapeDtypeStruct((40, K), F32)),
-        in_specs=[smem, hbm, hbm, hbm, hbm, hbm],
+        out_shape=shapes,
+        in_specs=[hbm, hbm, hbm, hbm, hbm, hbm],
         out_specs=(hbm, hbm),
         scratch_shapes=[
+            pltpu.SMEM((1,), jnp.int32),
             pltpu.VMEM((NC, BS, CH), F32),
             pltpu.VMEM((NC, CH, BS), F32),
             pltpu.VMEM((3, 2, BS, BS), BF16),
@@ -538,8 +522,8 @@
             pltpu.VMEM((1, K), F32), big(), big(), big(), big(), big(),
             pltpu.VMEM((BS, K), BF16),
             pltpu.VMEM((3, 8, K), F32),
-            pltpu.VMEM((3, COLS, 8, K), F32),
-            pltpu.VMEM((3, ROWS, 8, K), F32),
+            pltpu.VMEM((3, COLS - 1, 8, K), F32),
+            pltpu.VMEM((3, ROWS - 1, 8, K), F32),
             pltpu.VMEM((3, 8, K), F32),
             pltpu.VMEM((4, 4, 4, 40, K), F32),
             pltpu.VMEM((4, 4, 4, 40, K), F32),
@@ -548,17 +532,20 @@
             *[pltpu.VMEM((4, 4, size, K), F32) for _, size, _ in PARTS],
             *[pltpu.VMEM((4, size, K), F32) for _, size, _ in PARTS],
             pltpu.VMEM((40, K), F32),
-            dma((2,)), dma((NC,)), dma((NC,)), dma, dma((2,)),
-            dma((3, 4, NC)), dma((3, 4, NC)),
-            dma((3, 2, COLS)), dma((3, 2, COLS)),
-            dma((4,)), dma((4,)),
-            dma((3, 3, 4)), dma((3, 3, 4)),
-            dma((2, 4, 4)), dma((2, 4, 4)),
+            dma((3,)), dma((NC,)), dma((NC,)), dma, dma((2,)),
+            dma((7,)), dma((3, 2, NC)), dma((2, 2, NC)), dma((2,)),
+            dma((2,)), dma((3, 2)),
+            dma, dma((4,)),
+            dma((3, 3)), dma((3, 3)),
         ],
         compiler_params=pltpu.CompilerParams(
             collective_id=0, has_side_effects=True, vmem_limit_bytes=63 * 1024 * 1024
         ),
     )(band, marginal, penalty.reshape(1, K), ld_diag, ld_low, genotypes)
+    return pl.pallas_call(
+        copy_out,
+        out_shape=shapes,
+    )(*results)
 
 
 def solution(mesh):

time: 118 us -> 114 us (0.966)
  local copies, waits for them, and re-layouts: 3.2 us -> 0 us
    unnamed x2 -> x0, local copies, waits for them, and re-layouts: 3.2 us -> none
    pallas_call x1 -> x2, Pallas kernels: 114 us -> 113 us  [the longest x1 111 us: body(): pl.pallas_call(kernel, out_shape=shapes, in_specs=[hbm, hbm, hbm, hbm, hb...]
where the time goes in v4:
time: 114 us
  Pallas kernels  113 us (99%)
  between operations  1.29 us (1%)
    pallas_call x1, Pallas kernels, body(): pl.pallas_call(kernel, out_shape=shapes, in_specs=[hbm, hbm, hbm, hbm, hb...  111 us

profile of v4, /device:TPU:0, one launch (start us, length us, event | category | flops | bytes accessed | tf_op | source)
XLA Modules:
  0.0 114.2 jit_solution(12587588605833878507)
XLA Ops:
  1.3 111.1 %shard_map.77 = (f32[1024,128]{1,0:T(8,128)}, f32[40,128]{1,0:T(8,128)}) custom-call(s32[1]{0:T(128)S(6)} %copy.8.band_in, f32[1024,128]{1,0:T(8,128)} %marginal.1, f32[1,128]{1,0:T(1,128)} %bitcast.1, f32[1,1024,1024]{2,1,0:T(8,128)} %ld_diag.1, f32[1,2,1024,1024]{3,2,1,0:T(8,128)} %ld_low.1, bf16[5120,1024]{1,0:T(8,128)(2,1)} %genotypes.1), custom_call_target="tpu_custom_call" | custom-call | tf_op jit(solution)/shard_map/pallas_call | solution.py:506
  112.4 1.9 %shard_map.78 = (f32[1024,128]{1,0:T(8,128)}, f32[40,128]{1,0:T(8,128)}) custom-call(f32[1024,128]{1,0:T(8,128)} %get-tuple-element.4.effects_in, f32[40,128]{1,0:T(8,128)} %get-tuple-element.5.scores_in), custom_call_target="tpu_custom_call" | custom-call | tf_op jit(solution)/shard_map/pallas_call | solution.py:545

commit v5 on v4

--- a/solution.py
+++ b/solution.py
@@ -74,8 +74,7 @@
     def load(t, c):
         return pltpu.make_async_copy(ld_low.at[0, 1 - t, :, chunk(c)], stage.at[c], load_sem.at[c])
 
-    def load_diag(c):
-        return pltpu.make_async_copy(ld_diag.at[0, chunk(c)], diag_stage.at[c], diag_sem.at[c])
+    diag_copy = pltpu.make_async_copy(ld_diag.at[0], diag_stage, diag_sem)
 
     band_copy.start()
     b_copy.start()
@@ -133,8 +132,7 @@
     def _(c):
         send_own(0, c).start()
 
-    for c in range(NC):
-        load_diag(c).start()
+    diag_copy.start()
 
     place_f = [place >= distance for distance in (1, 2)]
     active = [
@@ -209,11 +207,13 @@
         )
 
     def diagonal(e):
+        if e == 0:
+            diag_copy.wait()
+
         @pl.loop(0, NC)
         def _(c):
             if e == 0:
-                load_diag(c).wait()
-                high, low = split(diag_stage[c])
+                high, low = split(diag_stage[chunk(c), :])
                 tiles[2, 0, chunk(c), :] = high
                 tiles[2, 1, chunk(c), :] = low
             dw[chunk(c), :] = (
@@ -328,6 +328,8 @@
     for c in (2, 3):
         send_onward(c).wait_recv()
         add_second(2, c)
+    send_on(2, 0).wait_recv()
+    add_second(2, 0)
     got = ar_sum(1, 1)
     rr, rd, dq, rq, qq = (got[j : j + 1] for j in range(5))
     a1 = rd / dq
@@ -346,8 +348,6 @@
     c1 = -a0 - a1 * (1.0 + b1) - b2 * a0
     c2 = a1 * a0
 
-    send_on(2, 0).wait_recv()
-    add_second(2, 0)
     send_on(2, 1).wait_recv()
     tail[...] = both(m2[2, chunk(1), :])
 
@@ -511,7 +511,7 @@
         scratch_shapes=[
             pltpu.SMEM((1,), jnp.int32),
             pltpu.VMEM((NC, BS, CH), F32),
-            pltpu.VMEM((NC, CH, BS), F32),
+            pltpu.VMEM((BS, BS), F32),
             pltpu.VMEM((3, 2, BS, BS), BF16),
             pltpu.VMEM((2, 2, BS, BS), BF16),
             pltpu.VMEM((8 * GROUP, BS), BF16),
@@ -532,7 +532,7 @@
             *[pltpu.VMEM((4, 4, size, K), F32) for _, size, _ in PARTS],
             *[pltpu.VMEM((4, size, K), F32) for _, size, _ in PARTS],
             pltpu.VMEM((40, K), F32),
-            dma((3,)), dma((NC,)), dma((NC,)), dma, dma((2,)),
+            dma((3,)), dma((NC,)), dma, dma, dma((2,)),
             dma((7,)), dma((3, 2, NC)), dma((2, 2, NC)), dma((2,)),
             dma((2,)), dma((3, 2)),
             dma, dma((4,)),

time: 114 us -> 114 us (level)
  no operation moved by 1% of the time
where the time goes in v5:
time: 114 us
  Pallas kernels  112 us (98%)
  between operations  1.29 us (1%)
    pallas_call x1, Pallas kernels, body(): pl.pallas_call(kernel, out_shape=shapes, in_specs=[hbm, hbm, hbm, hbm, hb...  111 us

profile of v5, /device:TPU:0, one launch (start us, length us, event | category | flops | bytes accessed | tf_op | source)
XLA Modules:
  0.0 113.8 jit_solution(4138314051370524365)
XLA Ops:
  1.3 110.6 %shard_map.77 = (f32[1024,128]{1,0:T(8,128)}, f32[40,128]{1,0:T(8,128)}) custom-call(s32[1]{0:T(128)S(6)} %copy.8.band_in, f32[1024,128]{1,0:T(8,128)} %marginal.1, f32[1,128]{1,0:T(1,128)} %bitcast.1, f32[1,1024,1024]{2,1,0:T(8,128)} %ld_diag.1, f32[1,2,1024,1024]{3,2,1,0:T(8,128)} %ld_low.1, bf16[5120,1024]{1,0:T(8,128)(2,1)} %genotypes.1), custom_call_target="tpu_custom_call" | custom-call | tf_op jit(solution)/shard_map/pallas_call | solution.py:506
  111.9 1.9 %shard_map.78 = (f32[1024,128]{1,0:T(8,128)}, f32[40,128]{1,0:T(8,128)}) custom-call(f32[1024,128]{1,0:T(8,128)} %get-tuple-element.4.effects_in, f32[40,128]{1,0:T(8,128)} %get-tuple-element.5.scores_in), custom_call_target="tpu_custom_call" | custom-call | tf_op jit(solution)/shard_map/pallas_call | solution.py:545
